TPU v7x, 256 devices: a whole 4x4x8 slice. The times are simulated.
256 devices in a mesh: section: 4 (over x), dp: 8 (over y, core), expert: 8 (over z).
Axes of the slice: x: 4, y: 4, z: 8, core: 2. Of those that a mesh axis runs over, the one named last changes fastest.
Arguments:
- patches: bfloat16 [32768, 1152], P(('dp', 'expert')), may hold values from -50 to 50
- lengths: int32 [64, 4], P(('dp', 'expert')), may hold values from 1 to 64, 128 in all within a row
- w_qkv: bfloat16 [1152, 3456], P(None, 'section'), may hold values from -4.714045 to 4.714045
- w_out: bfloat16 [1152, 1152], P('section'), may hold values from -0.1875 to 0.1875
- w_proj: bfloat16 [4608, 2048], P('dp', 'section'), may hold values from -0.09375 to 0.09375
- routes: int32 [8192, 6], P(('dp', 'expert')), may hold values from 0 to 63, all different within a row; in each aligned block of 128 rows (0 to 127, 128 to 255, ...) at most 24 rows name the same one
- gates: float32 [8192, 6], P(('dp', 'expert')), may hold values from 0.05 to 0.4
- w_gate: bfloat16 [64, 2048, 1408], P(('dp', 'expert'), None, 'section'), may hold values from -0.125 to 0.125
- w_up: bfloat16 [64, 2048, 1408], P(('dp', 'expert'), None, 'section'), may hold values from -0.125 to 0.125
- w_down: bfloat16 [64, 1408, 2048], P(('dp', 'expert'), 'section'), may hold values from -0.15625 to 0.15625
Outputs:
- language_out: bfloat16 [8192, 2048], P(('dp', 'expert'), 'section')
Inputs may be any that keep to these rules, and one draw needn't show every extreme that they name: Each row lists, in order, the lengths in merged tokens of a group's images; they sum to 128 and the largest is exactly 64. `routes`: A token's 6 experts differ. Among the rows of one device no expert is named more than 24 times, a bound that some block reaches in every draw.
All inputs are finite; a program needn't handle non-finite values.
Results may differ from a plain program's by a relative error of at most 0.012.
Values may be sent and summed in bfloat16 or wider, within the bound.
No kernel may reach another device: no remote copies, remote signals or barrier semaphores. Data moves between devices by JAX's collectives and lax.ppermute only.
A program may use at most 64 MiB of HBM per device.

v0:
```python
import functools
import math

import jax
import jax.numpy as jnp
from jax import lax
from jax.experimental import pallas as pl
from jax.experimental.pallas import tpu as pltpu
from jax.sharding import PartitionSpec as P


D_VIT = 1152
HEADS = 16
TOP = 6
BF = jnp.bfloat16
F32 = jnp.float32

LATE = 128
VMEM = pl.BlockSpec(memory_space=pltpu.VMEM)
SMEM = pl.BlockSpec(memory_space=pltpu.SMEM)


def params(mib):
    return pltpu.CompilerParams(vmem_limit_bytes=mib * 2**20)


def dot(a, b):
    return jnp.dot(a, b, preferred_element_type=F32)


def dot_tn(a, b):
    return lax.dot_general(a, b, (((0,), (0,)), ((), ())), preferred_element_type=F32)


def dot_nt(a, b):
    return lax.dot_general(a, b, (((1,), (1,)), ((), ())), preferred_element_type=F32)


def shift(value, axis, step):
    count = lax.axis_size(axis)
    return lax.ppermute(value, axis, [(i, (i + step) % count) for i in range(count)])


def partner(value):
    count = lax.axis_size("dp")
    return lax.ppermute(value, "dp", [(i, i ^ 1) for i in range(count)])


def layer_norm(values):
    center = values - jnp.mean(values, axis=-1, keepdims=True)
    spread = jnp.mean(center * center, axis=-1, keepdims=True)
    return center * lax.rsqrt(spread + 1e-06)


def route_tables(routes, gates, expert_total, capacity):
    rows = routes.shape[0]
    ids = jnp.arange(expert_total, dtype=jnp.int32)
    named = routes[:, :, None] == ids[None, None, :]
    member = jnp.any(named, axis=1)
    weight = jnp.sum(jnp.where(named, gates[:, :, None], 0.0), axis=1)
    places = jnp.arange(rows, dtype=jnp.int32)
    before = (places[:, None] > places[None, :]).astype(BF)
    slot = dot(before, member.astype(BF))
    slot = jnp.where(member, slot, 255.0).astype(BF)
    lanes = jnp.arange(expert_total * capacity, dtype=jnp.int32)
    spread = (lanes[None, :] // capacity == ids[:, None]).astype(BF)
    hit = dot(slot, spread) == (lanes % capacity).astype(F32)[None, :]
    pick = dot_tn(spread, slot.T) == (lanes % capacity).astype(F32)[:, None]
    high = weight.astype(BF)
    low = (weight - high.astype(F32)).astype(BF)
    gate_high = jnp.where(hit, dot(high, spread), 0.0).astype(BF)
    gate_low = jnp.where(hit, dot(low, spread), 0.0).astype(BF)
    return pick.astype(BF), jnp.concatenate([gate_high, gate_low], axis=0)


def project_body(place, patches, *refs):
    att, out_rows, rows, pick = refs[0:4], refs[4:8], refs[8:16], refs[16]
    own_out, late_out, slot_out = refs[17:20]
    att_v, out_v, proj_v, enc, sems = refs[20:]
    row_y, core = place[0], place[1]
    half = rows[0].shape[0]
    copies = []
    for d in range(4):
        copies.append(pltpu.make_async_copy(att[d], att_v.at[d], sems.at[d]))
        copies.append(pltpu.make_async_copy(out_rows[d], out_v.at[d], sems.at[4 + d]))
    for d in range(4):
        mine = pl.multiple_of(core * half, 64)
        other = pl.multiple_of((1 - core) * half, 64)
        copies.append(pltpu.make_async_copy(rows[d], proj_v.at[d, pl.ds(mine, half)], sems.at[8 + d]))
        copies.append(pltpu.make_async_copy(rows[4 + d], proj_v.at[d, pl.ds(other, half)], sems.at[12 + d]))
    for c in copies:
        c.start()
    for c in copies[:8]:
        c.wait()
    step = 128
    for r in range(patches.shape[0] // step):
        at = pl.ds(r * step, step)
        total = patches[at, :].astype(F32)
        for d in range(4):
            total += dot_tn(att_v[d, :, at], out_v[d])
        for q in range(enc.shape[0]):
            enc[q, at, :] = total[:, q * 128 : (q + 1) * 128]
    for c in copies[8:]:
        c.wait()
    merged = patches.shape[0] // 4
    acc = jnp.zeros(own_out.shape, F32)
    for d in range(4):
        j = lax.rem(row_y + 4 - d, 4)
        block = [enc[q, pl.ds(j, merged, stride=4), :].astype(BF) for q in range(enc.shape[0])]
        acc += dot(jnp.concatenate(block, axis=1), proj_v[d])
    own = acc.astype(BF)
    own_out[...] = own
    early = slot_out.shape[1]
    late_out[...] = own[:, early:]
    slot_out[...] = dot(pick[...], own[:, :early]).astype(BF)


def project(place, patches, att, out_rows, proj_rows, pick):
    merged = patches.shape[0] // 4
    columns = proj_rows[0].shape[1]
    half = proj_rows[0].shape[0]
    slots = pick.shape[0]
    anyspace = pl.BlockSpec(memory_space=pl.ANY)
    return pl.pallas_call(
        project_body,
        out_shape=(
            jax.ShapeDtypeStruct((merged, columns), BF),
            jax.ShapeDtypeStruct((merged, LATE), BF),
            jax.ShapeDtypeStruct((slots, columns - LATE), BF),
        ),
        in_specs=[SMEM, VMEM] + [anyspace] * 16 + [VMEM],
        out_specs=(VMEM, VMEM, VMEM),
        scratch_shapes=[
            pltpu.VMEM((4,) + att[0].shape, BF),
            pltpu.VMEM((4,) + out_rows[0].shape, BF),
            pltpu.VMEM((4, 2 * half, columns), BF),
            pltpu.VMEM((patches.shape[1] // 128, patches.shape[0], 128), F32),
            pltpu.SemaphoreType.DMA((16,)),
        ],
        compiler_params=params(24),
        name="project",
    )(place, patches, *att, *out_rows, *proj_rows, pick)


def pick_body(pick, late, out):
    out[...] = dot(pick[...], late[...]).astype(BF)


def pick_rows(pick, late):
    return pl.pallas_call(
        pick_body,
        out_shape=jax.ShapeDtypeStruct((pick.shape[0], late.shape[1]), BF),
        compiler_params=params(8),
        name="pick_rows",
    )(pick, late)


def squares(x):
    wide = x.astype(F32)
    wide = wide * wide
    return sum(wide[:, q * 128 : (q + 1) * 128] for q in range(x.shape[1] // 128))


def lanes_of(section, offset, sections, columns, width):
    return pl.ds(pl.multiple_of(lax.rem(section + offset, sections) * columns, 128), width)


ROWS = 256


def hbm(shape, dtype):
    return pltpu.MemorySpace.HBM(shape, dtype)


def keep(*values):
    return [pltpu.with_memory_space_constraint(v, pltpu.MemorySpace.HBM) for v in values]


def rows_spec(width, index=lambda r: (r, 0)):
    return pl.BlockSpec((ROWS, width), index)


def fixed_spec(value):
    return pl.BlockSpec(value.shape, lambda r: (0, 0), pipeline_mode=pl.Buffered(1))


def up_body(columns, sections, place, own, left, right, w, acc_out, square_out):
    width = own.shape[1]
    acc = jnp.zeros((ROWS, w.shape[0]), F32)
    square = jnp.zeros((ROWS, 128), F32)
    for o, piece in ((0, own), (3, left), (1, right)):
        x = piece[...]
        acc += dot_nt(x, w[:, lanes_of(place[0], o, sections, columns, width)])
        square += squares(x)
    acc_out[...] = acc
    square_out[...] = square


def up(columns, sections, place, own, left, right, w):
    rows, width = own.shape
    return pl.pallas_call(
        functools.partial(up_body, columns, sections),
        out_shape=(hbm((rows, w.shape[0]), F32), hbm((rows, 128), F32)),
        grid=(rows // ROWS,),
        in_specs=[SMEM] + [rows_spec(width)] * 3 + [fixed_spec(w)],
        out_specs=(rows_spec(w.shape[0]), rows_spec(128)),
        compiler_params=params(20),
        name="up",
    )(place, *keep(own, left, right, w))


def hidden_body(columns, sections, place, acc, square, late, far_a, far_b, w, w_late, w_down, hid_out, to_a, to_b):
    hidden_count = w_down.shape[0]
    width = far_a.shape[1]
    r, blocks = pl.program_id(0), pl.num_programs(0)
    in_a = r < blocks // 2
    x = jnp.where(in_a, far_a[...], far_b[...])
    y = late[...]
    two_away = lanes_of(place[0], 2, sections, columns, width)
    total = acc[...] + dot_nt(x, w[:, two_away])
    total += dot_nt(y, w_late[...])
    square_sum = square[...] + squares(x) + squares(y)
    mean = jnp.sum(square_sum, axis=-1, keepdims=True) * (1.0 / (columns * sections))
    row_scale = lax.rsqrt(mean + 1e-06)
    gate = total[:, :hidden_count] * row_scale
    upper = total[:, hidden_count:] * row_scale
    hidden = (gate / (1.0 + jnp.exp(-gate)) * upper).astype(BF)
    hid_out[...] = hidden
    part = dot(hidden, w_down[:, two_away]).astype(BF)

    @pl.when(in_a)
    def _():
        to_a[...] = part

    @pl.when(jnp.logical_not(in_a))
    def _():
        to_b[...] = part


def hidden_units(columns, sections, place, acc, square, late, far_a, far_b, w, w_late, w_down):
    rows, width = acc.shape[0], far_a.shape[1]
    half = rows // 2 // ROWS
    spec_a = rows_spec(width, lambda r: (jnp.minimum(r, half - 1), 0))
    spec_b = rows_spec(width, lambda r: (jnp.maximum(r - half, 0), 0))
    return pl.pallas_call(
        functools.partial(hidden_body, columns, sections),
        out_shape=(hbm((rows, w_down.shape[0]), BF), hbm((rows // 2, width), BF), hbm((rows // 2, width), BF)),
        grid=(rows // ROWS,),
        in_specs=[SMEM, rows_spec(acc.shape[1]), rows_spec(128), rows_spec(late.shape[1]), spec_a, spec_b]
        + [fixed_spec(w), fixed_spec(w_late), fixed_spec(w_down)],
        out_specs=(rows_spec(w_down.shape[0]), spec_a, spec_b),
        compiler_params=params(24),
        name="hidden_units",
    )(place, *keep(acc, square, late, far_a, far_b, w, w_late, w_down))


def down_body(columns, sections, place, hidden, w_down, w_late, right_out, left_out, here_out, late_out):
    width = here_out.shape[1]
    h = hidden[...]
    for o, out in ((1, right_out), (3, left_out), (0, here_out)):
        out[...] = dot(h, w_down[:, lanes_of(place[0], o, sections, columns, width)]).astype(BF)
    late_out[...] = dot(h, w_late[...]).astype(BF)


def down(columns, sections, place, hidden, w_down, w_late):
    rows = hidden.shape[0]
    widths = [columns - LATE] * 3 + [LATE * sections]
    return pl.pallas_call(
        functools.partial(down_body, columns, sections),
        out_shape=[hbm((rows, n), BF) for n in widths],
        grid=(rows // ROWS,),
        in_specs=[SMEM, rows_spec(hidden.shape[1]), fixed_spec(w_down), fixed_spec(w_late)],
        out_specs=[rows_spec(n) for n in widths],
        compiler_params=params(16),
        name="down",
    )(place, *keep(hidden, w_down, w_late))


def weigh_body(gates, late, out):
    both = dot(gates[...], late[...])
    merged = both.shape[0] // 2
    total = (both[:merged] + both[merged:]).astype(BF)
    for s in range(out.shape[0]):
        out[s] = total[:, s * LATE : (s + 1) * LATE]


def weigh(gates, late, sections):
    return pl.pallas_call(
        weigh_body,
        out_shape=jax.ShapeDtypeStruct((sections, gates.shape[0] // 2, LATE), BF),
        compiler_params=params(12),
        name="weigh",
    )(gates, late)


def combine_body(gates, own, late, early, out):
    merged, _ = own.shape
    width = early.shape[1]
    both = dot(gates[...], early[...])
    out[:, :width] = (own[:, :width].astype(F32) + both[:merged] + both[merged:]).astype(BF)
    total = own[:, width:].astype(F32)
    for s in range(late.shape[0]):
        total += late[s].astype(F32)
    out[:, width:] = total.astype(BF)


def combine(gates, own, late, early):
    return pl.pallas_call(
        combine_body,
        out_shape=jax.ShapeDtypeStruct(own.shape, BF),
        compiler_params=params(12),
        name="combine",
    )(gates, own, late, early)


def per_device(patches, lengths, w_qkv, w_out, w_proj, routes, gates, w_gate, w_up, w_down):
    data_count = lax.axis_size("dp")
    owner_count = lax.axis_size("expert")
    sections = lax.axis_size("section")
    patch_rows, _ = patches.shape
    merged_count = patch_rows // 4
    head_dim = D_VIT // HEADS
    local_heads = w_qkv.shape[1] // (3 * head_dim)
    scale = 1.0 / math.sqrt(head_dim)
    expert_total = data_count * owner_count
    capacity = max(2, min(merged_count, 2 * merged_count * TOP // expert_total))
    columns = w_proj.shape[1]
    early = columns - LATE
    place = jnp.stack([lax.axis_index("section")]).astype(jnp.int32)
    dp_place = jnp.stack([lax.axis_index("dp") // 2, lax.axis_index("dp") % 2]).astype(jnp.int32)

    out_rows, mine = [w_out], [w_proj]
    for d in (1, 2, 3):
        mine.append(shift(w_proj, "dp", 2 * d))
        out_rows.append(shift(w_out, "section", d))
    proj_rows = mine + [partner(m) for m in mine]

    normed_in = layer_norm(patches.astype(F32)).astype(BF)
    packed = dot(normed_in, w_qkv).astype(BF)
    packed = packed.reshape(patch_rows, local_heads, 3, head_dim)
    query = packed[:, :, 0]
    key_part = packed[:, :, 1]
    value_part = packed[:, :, 2]
    ends = jnp.cumsum(lengths[0]) * 4
    places = jnp.arange(patch_rows, dtype=jnp.int32)
    segment = jnp.sum((places[:, None] >= ends[None, :]).astype(jnp.int32), axis=1)
    same = segment[:, None] == segment[None, :]
    scores = jnp.einsum("qhd,khd->hqk", query, key_part, preferred_element_type=F32) * scale
    scores = jnp.where(same[None], scores, -jnp.inf)
    peak = jnp.max(scores, axis=-1, keepdims=True)
    weights = jnp.where(same[None], jnp.exp(scores - peak), 0.0)
    probs = (weights / jnp.sum(weights, axis=-1, keepdims=True)).astype(BF)
    attended = jnp.einsum("hqk,khd->hdq", probs, value_part, preferred_element_type=F32)
    attended = attended.astype(BF).reshape(local_heads * head_dim, patch_rows)

    att = [attended]
    for d in (1, 2, 3):
        att.append(shift(attended, "section", d))
    pick, gate_rows = route_tables(routes, gates, expert_total, capacity)
    w_both = jnp.concatenate([w_gate[0].T, w_up[0].T], axis=0)
    last = lambda w: jnp.concatenate([w[:, s * columns + early : (s + 1) * columns] for s in range(sections)], axis=1)
    w_late, down_late = last(w_both), last(w_down[0])
    proj_own, late, outgoing = project(dp_place, patches, att, out_rows, proj_rows, pick)

    rows = expert_total * capacity

    def exchange(value):
        wide = value.reshape(expert_total, capacity, value.shape[1])
        wide = lax.all_to_all(wide, ("dp", "expert"), split_axis=0, concat_axis=0, tiled=True)
        return wide.reshape(value.shape)

    own = exchange(outgoing)
    late_all = lax.all_gather(late, "section", axis=1, tiled=True)
    late_rows = pick_rows(pick, late_all)
    late_rows = exchange(late_rows)
    left = shift(own, "section", 1)
    right = shift(own, "section", -1)
    far_a = shift(left[: rows // 2], "section", 1)
    far_b = shift(right[rows // 2 :], "section", -1)
    acc, square = up(columns, sections, place, own, left, right, w_both)
    hidden, to_a, to_b = hidden_units(
        columns, sections, place, acc, square, late_rows, far_a, far_b, w_both, w_late, w_down[0]
    )
    via_a = shift(to_a, "section", 1)
    via_b = shift(to_b, "section", -1)
    to_right, to_left, here, late_out = down(columns, sections, place, hidden, w_down[0], down_late)
    late_back = exchange(late_out)
    top, bottom = to_right[: rows // 2], to_right[rows // 2 :]
    to_right = jnp.concatenate([(top.astype(F32) + via_a.astype(F32)).astype(BF), bottom], axis=0)
    top, bottom = to_left[: rows // 2], to_left[rows // 2 :]
    to_left = jnp.concatenate([top, (bottom.astype(F32) + via_b.astype(F32)).astype(BF)], axis=0)
    from_left = shift(to_right, "section", 1)
    from_right = shift(to_left, "section", -1)
    total = (here.astype(F32) + from_left.astype(F32) + from_right.astype(F32)).astype(BF)
    returned = exchange(total)
    late_sum = weigh(gate_rows, late_back, sections)
    late_sum = lax.all_to_all(late_sum, "section", split_axis=0, concat_axis=0, tiled=True)
    return combine(gate_rows, proj_own, late_sum, returned)


def solution(mesh):
    return jax.shard_map(
        per_device,
        mesh=mesh,
        in_specs=(
            P(("dp", "expert"), None),
            P(("dp", "expert"), None),
            P(None, "section"),
            P("section", None),
            P("dp", "section"),
            P(("dp", "expert"), None),
            P(("dp", "expert"), None),
            P(("dp", "expert"), None, "section"),
            P(("dp", "expert"), None, "section"),
            P(("dp", "expert"), "section", None),
        ),
        out_specs=P(("dp", "expert"), "section"),
        check_vma=False,
    )
```

profile of v0, /device:TPU:8, one launch (start us, length us, event | category | flops | bytes accessed | tf_op | source)
XLA Modules:
  0.0 305.9 jit_solution(6189759146609860667)
XLA Ops:
  2.7 2.5 convolution_convert_fusion
  5.2 5.0 %fusion.43 = (f32[4,512]{1,0:T(4,128)S(1)}, f32[4,512,512]{1,2,0:T(8,128)}) fusion(pred[512,512]{0,1:T(8,128)(4,1)S(1)} %broadcast_compare_fusion, bf16[512,4,3,72]{0,3,2,1:T(8,128)(2,1)} %bitcast.75), kind=kOutput, calls=%fused_computation.88 | convolution fusion | flops 156238336 | bytes 5316608 | tf_op jit(solution)/shard_map/sub | solution.py:351
  10.2 2.8 fusion.13
  14.6 2.7 collective-permute-start.1
  20.9 8.5 %collective-permute-done.refs_1_ = bf16[288,512]{1,0:T(8,128)(2,1)S(1)} collective-permute-done((bf16[288,512]{1,0:T(8,128)(2,1)S(1)}, bf16[288,512]{1,0:T(8,128)(2,1)S(1)}, u32[]{:S(2)}, u32[]{:S(2)}) %collective-permute-start) | collective-permute-done | bytes 294944 | tf_op jit(solution)/shard_map/ppermute | solution.py:41
  30.2 2.3 collective-permute-start.7
  35.8 2.3 collective-permute-start.4
  38.2 8.6 %collective-permute-done.7.refs_10_ = bf16[576,512]{1,0:T(8,128)(2,1)} collective-permute-done((bf16[576,512]{1,0:T(8,128)(2,1)}, bf16[576,512]{1,0:T(8,128)(2,1)}, u32[]{:S(2)}, u32[]{:S(2)}) %collective-permute-start.7) | collective-permute-done | bytes 589856 | tf_op jit(solution)/shard_map/ppermute | solution.py:41
  46.7 5.7 %collective-permute-done.8.refs_11_ = bf16[576,512]{1,0:T(8,128)(2,1)} collective-permute-done((bf16[576,512]{1,0:T(8,128)(2,1)}, bf16[576,512]{1,0:T(8,128)(2,1)}, u32[]{:S(2)}, u32[]{:S(2)}) %collective-permute-start.8) | collective-permute-done | bytes 589856 | tf_op jit(solution)/shard_map/ppermute | solution.py:41
  53.8 5.0 %collective-permute-done.4.refs_6_ = bf16[288,1152]{1,0:T(8,128)(2,1)S(1)} collective-permute-done((bf16[288,1152]{1,0:T(8,128)(2,1)}, bf16[288,1152]{1,0:T(8,128)(2,1)S(1)}, u32[]{:S(2)}, u32[]{:S(2)}) %collective-permute-start.4) | collective-permute-done | bytes 663584 | tf_op jit(solution)/shard_map/ppermute | solution.py:41
  58.8 6.4 %collective-permute-done.5.refs_7_ = bf16[288,1152]{1,0:T(8,128)(2,1)S(1)} collective-permute-done((bf16[288,1152]{1,0:T(8,128)(2,1)}, bf16[288,1152]{1,0:T(8,128)(2,1)S(1)}, u32[]{:S(2)}, u32[]{:S(2)}) %collective-permute-start.5) | collective-permute-done | bytes 663584 | tf_op jit(solution)/shard_map/ppermute | solution.py:41
  68.1 6.3 %project.1 = (bf16[128,512]{1,0:T(8,128)(2,1)S(1)}, bf16[128,128]{1,0:T(8,128)(2,1)S(1)}, bf16[1536,384]{1,0:T(8,128)(2,1)S(1)}) custom-call(s32[2]{0:T(128)S(1)} %pad_add_fusion.place, bf16[512,1152]{1,0:T(8,128)(2,1)S(1)} %copy-done.1, bf16[288,512]{1,0:T(8,128)(2,1)S(1)} %bitcast.64, bf16[288,512]{1,0:T(8,128)(2,1)S(1)} %copy-done.7, ...), custom_call_target="tpu_custom_call" | custom-call | tf_op jit(solution)/shard_map/project/pallas_call | solution.py:124
  76.2 15.6 %all-to-all-start = ((bf16[64,24,384]{2,1,0:T(8,128)(2,1)}), bf16[64,24,384]{2,1,0:T(8,128)(2,1)}, u32[]{:S(2)}, u32[]{:S(2)}) async-start(bf16[64,24,384]{2,1,0:T(8,128)(2,1)} %bitcast.60), calls=%async_computation | async-start | bytes 2359296 | tf_op jit(solution)/shard_map/all_to_all | solution.py:369
  91.8 11.1 %all_gather.3.late = bf16[128,512]{1,0:T(8,128)(2,1)S(1)} all-gather(bf16[128,128]{1,0:T(8,128)(2,1)S(1)} %get-tuple-element.21), channel_id=1, replica_groups=mesh['section'=4,'dp'=8,'expert'=8] {'section'}, dimensions={1}, use_global_device_ids=true | all-gather | bytes 163840 | tf_op jit(solution)/shard_map/all_gather | solution.py:373
  104.6 18.3 %all-to-all-done = bf16[64,24,384]{2,1,0:T(8,128)(2,1)} async-done(((bf16[64,24,384]{2,1,0:T(8,128)(2,1)}), bf16[64,24,384]{2,1,0:T(8,128)(2,1)}, u32[]{:S(2)}, u32[]{:S(2)}) %all-to-all-start) | async-done | bytes 1179680 | tf_op jit(solution)/shard_map/all_to_all | solution.py:369
  122.9 6.7 %all-to-all-start.1 = ((bf16[64,24,512]{2,1,0:T(8,128)(2,1)}), bf16[64,24,512]{2,1,0:T(8,128)(2,1)}, u32[]{:S(2)}, u32[]{:S(2)}) async-start(bf16[64,24,512]{2,1,0:T(8,128)(2,1)} %bitcast.58), calls=%async_computation.1 | async-start | bytes 3145728 | tf_op jit(solution)/shard_map/all_to_all | solution.py:369
  130.0 3.4 %collective-permute-start.14 = (bf16[1536,384]{1,0:T(8,128)(2,1)}, bf16[1536,384]{1,0:T(8,128)(2,1)S(1)}, u32[]{:S(2)}, u32[]{:S(2)}) collective-permute-start(bf16[1536,384]{1,0:T(8,128)(2,1)} %bitcast.11.own), channel_id=1, source_target_pairs={{0,192},{64,0},{128,64},{192,128},{1,193},{65,1},{129,65},{193,129... | collective-permute-start | bytes 3538952 | tf_op jit(solution)/shard_map/ppermute | solution.py:41
  134.4 25.3 %collective-permute-done.13.left = bf16[1536,384]{1,0:T(8,128)(2,1)S(1)} collective-permute-done((bf16[1536,384]{1,0:T(8,128)(2,1)}, bf16[1536,384]{1,0:T(8,128)(2,1)S(1)}, u32[]{:S(2)}, u32[]{:S(2)}) %collective-permute-start.13) | collective-permute-done | bytes 1179680 | tf_op jit(solution)/shard_map/ppermute | solution.py:41
  163.6 3.2 %collective-permute-start.16 = (bf16[768,384]{1,0:T(8,128)(2,1)}, bf16[768,384]{1,0:T(8,128)(2,1)}, u32[]{:S(2)}, u32[]{:S(2)}) collective-permute-start(bf16[768,384]{1,0:T(8,128)(2,1)} %slice.72), channel_id=1, source_target_pairs={{0,192},{64,0},{128,64},{192,128},{1,193},{65,1},{129,65},{193,129... | collective-permute-start | bytes 1769480 | tf_op jit(solution)/shard_map/ppermute | solution.py:41
  170.4 1.8 pad_maximum_fusion.w
  172.2 9.2 %up.1 = (f32[1536,704]{1,0:T(8,128)}, f32[1536,128]{1,0:T(8,128)}) custom-call(s32[1]{0:T(128)} %bitcast.9.place, bf16[1536,384]{1,0:T(8,128)(2,1)} %bitcast.11.own, bf16[1536,384]{1,0:T(8,128)(2,1)} %copy-done.16, bf16[1536,384]{1,0:T(8,128)(2,1)} %copy-done.17, bf16[704,2048]{1,0:T(8,128)(2,1)} %pad_maximum_fusion.w), custom_call_target="tpu_custom_call" | custom-call | tf_op jit(solution)/shard_map/up/pallas_call | solution.py:201
  181.5 11.6 %hidden_units.1 = (bf16[1536,352]{1,0:T(8,128)(2,1)}, bf16[768,384]{1,0:T(8,128)(2,1)}, bf16[768,384]{1,0:T(8,128)(2,1)}) custom-call(s32[1]{0:T(128)} %bitcast.9.place, f32[1536,704]{1,0:T(8,128)} %get-tuple-element.19.acc, f32[1536,128]{1,0:T(8,128)} %get-tuple-element.20.square, bf16[1536,512]{1,0:T(8,128)(2,1)} %bitcast.17.late, ...), custom_call_target="tpu_custom_call" | custom-call | tf_op jit(solution)/shard_map/hidden_units/pallas_call | solution.py:245
  193.0 7.2 %down.1 = (bf16[1536,384]{1,0:T(8,128)(2,1)}, bf16[1536,384]{1,0:T(8,128)(2,1)}, bf16[1536,384]{1,0:T(8,128)(2,1)}, bf16[1536,512]{1,0:T(8,128)(2,1)}) custom-call(s32[1]{0:T(128)} %bitcast.9.place, bf16[1536,352]{1,0:T(8,128)(2,1)} %get-tuple-element.22.hidden, bf16[352,2048]{1,0:T(8,128)(2,1)} %bitcast.67, bf16[352,512]{1,0:T(8,128)(2,1)} %pad_maximum_fusion.5.w_late), custom_call_target="tpu_custom_call" | custom-call | tf_op jit(solution)/shard_map/down/pallas_call | solution.py:268
  200.2 10.6 %all-to-all-start.2 = ((bf16[64,24,512]{2,1,0:T(8,128)(2,1)}), bf16[64,24,512]{2,1,0:T(8,128)(2,1)}, u32[]{:S(2)}, u32[]{:S(2)}) async-start(bf16[64,24,512]{2,1,0:T(8,128)(2,1)} %bitcast.73), calls=%async_computation.2 | async-start | bytes 3145728 | tf_op jit(solution)/shard_map/all_to_all | solution.py:369
  210.9 3.2 %collective-permute-start.19 = (bf16[768,384]{1,0:T(8,128)(2,1)}, bf16[768,384]{1,0:T(8,128)(2,1)S(1)}, u32[]{:S(2)}, u32[]{:S(2)}) collective-permute-start(bf16[768,384]{1,0:T(8,128)(2,1)} %get-tuple-element.28), channel_id=1, source_target_pairs={{0,192},{64,0},{128,64},{192,128},{1,193},{65,1},{129,65},{193,129... | collective-permute-start | bytes 1769480 | tf_op jit(solution)/shard_map/ppermute | solution.py:41
  215.4 12.4 %collective-permute-done.17 = bf16[768,384]{1,0:T(8,128)(2,1)S(1)} collective-permute-done((bf16[768,384]{1,0:T(8,128)(2,1)}, bf16[768,384]{1,0:T(8,128)(2,1)S(1)}, u32[]{:S(2)}, u32[]{:S(2)}) %collective-permute-start.17) | collective-permute-done | bytes 589856 | tf_op jit(solution)/shard_map/ppermute | solution.py:41
  230.5 3.2 %collective-permute-start.20 = (bf16[1536,384]{1,0:T(8,128)(2,1)}, bf16[1536,384]{1,0:T(8,128)(2,1)}, u32[]{:S(2)}, u32[]{:S(2)}) collective-permute-start(bf16[1536,384]{1,0:T(8,128)(2,1)} %pad_maximum_fusion.2), channel_id=1, source_target_pairs={{0,192},{64,0},{128,64},{192,128},{1,193},{65,1},{129,65},{193,129... | collective-permute-start | bytes 3538952 | tf_op jit(solution)/shard_map/ppermute | solution.py:41
  234.7 15.6 %all-to-all-done.2 = bf16[64,24,512]{2,1,0:T(8,128)(2,1)} async-done(((bf16[64,24,512]{2,1,0:T(8,128)(2,1)}), bf16[64,24,512]{2,1,0:T(8,128)(2,1)}, u32[]{:S(2)}, u32[]{:S(2)}) %all-to-all-start.2) | async-done | bytes 1572896 | tf_op jit(solution)/shard_map/all_to_all | solution.py:369
  250.2 2.6 weigh.1
  252.8 3.3 %all-to-all-start.3 = ((bf16[4,128,128]{2,1,0:T(8,128)(2,1)}), bf16[4,128,128]{2,1,0:T(8,128)(2,1)S(1)}, u32[]{:S(2)}, u32[]{:S(2)}) async-start(bf16[4,128,128]{2,1,0:T(8,128)(2,1)} %weigh.1), calls=%async_computation.3 | async-start | bytes 262144 | tf_op jit(solution)/shard_map/all_to_all | solution.py:397
  259.2 3.4 %add_convert_fusion = bf16[1536,384]{1,0:T(8,128)(2,1)} fusion(bf16[1536,384]{1,0:T(8,128)(2,1)} %collective-permute-done.20, bf16[1536,384]{1,0:T(8,128)(2,1)} %collective-permute-done.18, bf16[1536,384]{1,0:T(8,128)(2,1)} %get-tuple-element.24), kind=kLoop, calls=%fused_computation.26 | loop fusion | flops 3538944 | bytes 4718592 | tf_op jit(solution)/shard_map/convert_element_type | solution.py:394
  262.7 42.0 %all_to_all.25 = bf16[64,24,384]{2,1,0:T(8,128)(2,1)S(1)} all-to-all(bf16[64,24,384]{2,1,0:T(8,128)(2,1)} %bitcast.72), channel_id=1, replica_groups=mesh['section'=4,'dp'=8,'expert'=8] {'dp','expert'}, dimensions={0} | all-to-all | bytes 2359296 | tf_op jit(solution)/shard_map/all_to_all | solution.py:369
  (108 shorter events, 37.6 us)
Async XLA Ops:
  10.2 42.9 %copy-start.20 = (s32[128,6]{0,1:T(8,128)S(1)}, s32[128,6]{0,1:T(8,128)}, u32[]{:S(2)}) copy-start(s32[128,6]{0,1:T(8,128)} %param.15) | copy-start | bytes 9220
  13.0 16.4 %collective-permute-start = (bf16[288,512]{1,0:T(8,128)(2,1)S(1)}, bf16[288,512]{1,0:T(8,128)(2,1)S(1)}, u32[]{:S(2)}, u32[]{:S(2)}) collective-permute-start(bf16[288,512]{1,0:T(8,128)(2,1)S(1)} %bitcast.61), channel_id=1, source_target_pairs={{0,64},{64,128},{128,192},{192,0},{1,65},{65,129},{129,193},{193,1... | collective-permute-start | bytes 884744 | tf_op jit(solution)/shard_map/ppermute | solution.py:41
  14.6 17.9 %collective-permute-start.1 = (bf16[288,512]{1,0:T(8,128)(2,1)S(1)}, bf16[288,512]{1,0:T(8,128)(2,1)S(1)}, u32[]{:S(2)}, u32[]{:S(2)}) collective-permute-start(bf16[288,512]{1,0:T(8,128)(2,1)S(1)} %bitcast.62), channel_id=1, source_target_pairs={{0,128},{64,192},{128,0},{192,64},{1,129},{65,193},{129,1},{193,65... | collective-permute-start | bytes 884744 | tf_op jit(solution)/shard_map/ppermute | solution.py:41
  17.3 17.2 %collective-permute-start.2 = (bf16[288,512]{1,0:T(8,128)(2,1)S(1)}, bf16[288,512]{1,0:T(8,128)(2,1)S(1)}, u32[]{:S(2)}, u32[]{:S(2)}) collective-permute-start(bf16[288,512]{1,0:T(8,128)(2,1)S(1)} %bitcast.63), channel_id=1, source_target_pairs={{0,192},{64,0},{128,64},{192,128},{1,193},{65,1},{129,65},{193,129... | collective-permute-start | bytes 884744 | tf_op jit(solution)/shard_map/ppermute | solution.py:41
  18.7 34.2 %collective-permute-start.3 = (bf16[288,1152]{1,0:T(8,128)(2,1)}, bf16[288,1152]{1,0:T(8,128)(2,1)}, u32[]{:S(2)}, u32[]{:S(2)}) collective-permute-start(bf16[288,1152]{1,0:T(8,128)(2,1)} %refs_4_.1), channel_id=1, source_target_pairs={{0,64},{64,128},{128,192},{192,0},{1,65},{65,129},{129,193},{193,1... | collective-permute-start | bytes 1990664 | tf_op jit(solution)/shard_map/ppermute | solution.py:41
  19.3 16.5 %collective-permute-start.6 = (bf16[576,512]{1,0:T(8,128)(2,1)}, bf16[576,512]{1,0:T(8,128)(2,1)}, u32[]{:S(2)}, u32[]{:S(2)}) collective-permute-start(bf16[576,512]{1,0:T(8,128)(2,1)} %refs_8_.1), channel_id=1, source_target_pairs={{0,16},{8,24},{16,32},{24,40},{32,48},{40,56},{48,0},{56,8},{1,17}... | collective-permute-start | bytes 1769480 | tf_op jit(solution)/shard_map/ppermute | solution.py:41
  30.2 16.6 %collective-permute-start.7 = (bf16[576,512]{1,0:T(8,128)(2,1)}, bf16[576,512]{1,0:T(8,128)(2,1)}, u32[]{:S(2)}, u32[]{:S(2)}) collective-permute-start(bf16[576,512]{1,0:T(8,128)(2,1)} %refs_8_.1), channel_id=1, source_target_pairs={{0,32},{8,40},{16,48},{24,56},{32,0},{40,8},{48,16},{56,24},{1,33}... | collective-permute-start | bytes 1769480 | tf_op jit(solution)/shard_map/ppermute | solution.py:41
  33.2 19.3 %collective-permute-start.8 = (bf16[576,512]{1,0:T(8,128)(2,1)}, bf16[576,512]{1,0:T(8,128)(2,1)}, u32[]{:S(2)}, u32[]{:S(2)}) collective-permute-start(bf16[576,512]{1,0:T(8,128)(2,1)} %refs_8_.1), channel_id=1, source_target_pairs={{0,48},{8,56},{16,0},{24,8},{32,16},{40,24},{48,32},{56,40},{1,49}... | collective-permute-start | bytes 1769480 | tf_op jit(solution)/shard_map/ppermute | solution.py:41
  35.2 17.2 %collective-permute-start.9 = (bf16[576,512]{1,0:T(8,128)(2,1)}, bf16[576,512]{1,0:T(8,128)(2,1)}, u32[]{:S(2)}, u32[]{:S(2)}) collective-permute-start(bf16[576,512]{1,0:T(8,128)(2,1)} %refs_8_.1), channel_id=1, source_target_pairs={{0,8},{8,0},{16,24},{24,16},{32,40},{40,32},{48,56},{56,48},{1,9},... | collective-permute-start | bytes 1769480 | tf_op jit(solution)/shard_map/ppermute | solution.py:46
  35.8 23.0 %collective-permute-start.4 = (bf16[288,1152]{1,0:T(8,128)(2,1)}, bf16[288,1152]{1,0:T(8,128)(2,1)S(1)}, u32[]{:S(2)}, u32[]{:S(2)}) collective-permute-start(bf16[288,1152]{1,0:T(8,128)(2,1)} %refs_4_.1), channel_id=1, source_target_pairs={{0,128},{64,192},{128,0},{192,64},{1,129},{65,193},{129,1},{193,65... | collective-permute-start | bytes 1990664 | tf_op jit(solution)/shard_map/ppermute | solution.py:41
  46.7 18.5 %collective-permute-start.5 = (bf16[288,1152]{1,0:T(8,128)(2,1)}, bf16[288,1152]{1,0:T(8,128)(2,1)S(1)}, u32[]{:S(2)}, u32[]{:S(2)}) collective-permute-start(bf16[288,1152]{1,0:T(8,128)(2,1)} %refs_4_.1), channel_id=1, source_target_pairs={{0,192},{64,0},{128,64},{192,128},{1,193},{65,1},{129,65},{193,129... | collective-permute-start | bytes 1990664 | tf_op jit(solution)/shard_map/ppermute | solution.py:41
  52.4 12.8 %collective-permute-start.10 = (bf16[576,512]{1,0:T(8,128)(2,1)}, bf16[576,512]{1,0:T(8,128)(2,1)S(1)}, u32[]{:S(2)}, u32[]{:S(2)}) collective-permute-start(bf16[576,512]{1,0:T(8,128)(2,1)} %collective-permute-done.6.refs_9_), channel_id=1, source_target_pairs={{0,8},{8,0},{16,24},{24,16},{32,40},{40,32},{48,56},{56,48},{1,9},... | collective-permute-start | bytes 1769480 | tf_op jit(solution)/shard_map/ppermute | solution.py:46
  52.4 12.8 %collective-permute-start.11 = (bf16[576,512]{1,0:T(8,128)(2,1)}, bf16[576,512]{1,0:T(8,128)(2,1)S(1)}, u32[]{:S(2)}, u32[]{:S(2)}) collective-permute-start(bf16[576,512]{1,0:T(8,128)(2,1)} %collective-permute-done.7.refs_10_), channel_id=1, source_target_pairs={{0,8},{8,0},{16,24},{24,16},{32,40},{40,32},{48,56},{56,48},{1,9},... | collective-permute-start | bytes 1769480 | tf_op jit(solution)/shard_map/ppermute | solution.py:46
  52.9 12.3 %collective-permute-start.12 = (bf16[576,512]{1,0:T(8,128)(2,1)}, bf16[576,512]{1,0:T(8,128)(2,1)S(1)}, u32[]{:S(2)}, u32[]{:S(2)}) collective-permute-start(bf16[576,512]{1,0:T(8,128)(2,1)} %collective-permute-done.8.refs_11_), channel_id=1, source_target_pairs={{0,8},{8,0},{16,24},{24,16},{32,40},{40,32},{48,56},{56,48},{1,9},... | collective-permute-start | bytes 1769480 | tf_op jit(solution)/shard_map/ppermute | solution.py:46
  53.8 20.7 %copy-start.3 = (bf16[1536,128]{1,0:T(8,128)(2,1)}, bf16[1536,128]{1,0:T(8,128)(2,1)S(1)}, u32[]{:S(2)}) copy-start(bf16[1536,128]{1,0:T(8,128)(2,1)S(1)} %fusion.8.refs_16_.pick) | copy-start | bytes 1179652
  76.2 26.8 %copy-start.4 = (bf16[1536,128]{1,0:T(8,128)(2,1)S(1)}, bf16[1536,128]{1,0:T(8,128)(2,1)}, u32[]{:S(2)}) copy-start(bf16[1536,128]{1,0:T(8,128)(2,1)} %copy-done.3) | copy-start | bytes 1179652
  76.2 46.8 %all-to-all-start = ((bf16[64,24,384]{2,1,0:T(8,128)(2,1)}), bf16[64,24,384]{2,1,0:T(8,128)(2,1)}, u32[]{:S(2)}, u32[]{:S(2)}) async-start(bf16[64,24,384]{2,1,0:T(8,128)(2,1)} %bitcast.60), calls=%async_computation | async-start | bytes 2359296 | tf_op jit(solution)/shard_map/all_to_all | solution.py:369
  122.9 58.5 %all-to-all-start.1 = ((bf16[64,24,512]{2,1,0:T(8,128)(2,1)}), bf16[64,24,512]{2,1,0:T(8,128)(2,1)}, u32[]{:S(2)}, u32[]{:S(2)}) async-start(bf16[64,24,512]{2,1,0:T(8,128)(2,1)} %bitcast.58), calls=%async_computation.1 | async-start | bytes 3145728 | tf_op jit(solution)/shard_map/all_to_all | solution.py:369
  129.6 30.2 %collective-permute-start.13 = (bf16[1536,384]{1,0:T(8,128)(2,1)}, bf16[1536,384]{1,0:T(8,128)(2,1)S(1)}, u32[]{:S(2)}, u32[]{:S(2)}) collective-permute-start(bf16[1536,384]{1,0:T(8,128)(2,1)} %bitcast.11.own), channel_id=1, source_target_pairs={{0,64},{64,128},{128,192},{192,0},{1,65},{65,129},{129,193},{193,1... | collective-permute-start | bytes 3538952 | tf_op jit(solution)/shard_map/ppermute | solution.py:41
  130.0 31.8 %collective-permute-start.14 = (bf16[1536,384]{1,0:T(8,128)(2,1)}, bf16[1536,384]{1,0:T(8,128)(2,1)S(1)}, u32[]{:S(2)}, u32[]{:S(2)}) collective-permute-start(bf16[1536,384]{1,0:T(8,128)(2,1)} %bitcast.11.own), channel_id=1, source_target_pairs={{0,192},{64,0},{128,64},{192,128},{1,193},{65,1},{129,65},{193,129... | collective-permute-start | bytes 3538952 | tf_op jit(solution)/shard_map/ppermute | solution.py:41
  134.4 33.2 %copy-start.14 = (bf16[1,2048,352]{1,2,0:T(8,128)(2,1)S(1)}, bf16[1,2048,352]{1,2,0:T(8,128)(2,1)}, u32[]{:S(2)}) copy-start(bf16[1,2048,352]{1,2,0:T(8,128)(2,1)} %param.18) | copy-start | bytes 4325380
  161.7 19.7 %collective-permute-start.15 = (bf16[768,384]{1,0:T(8,128)(2,1)}, bf16[768,384]{1,0:T(8,128)(2,1)}, u32[]{:S(2)}, u32[]{:S(2)}) collective-permute-start(bf16[768,384]{1,0:T(8,128)(2,1)} %slice.71), channel_id=1, source_target_pairs={{0,64},{64,128},{128,192},{192,0},{1,65},{65,129},{129,193},{193,1... | collective-permute-start | bytes 1769480 | tf_op jit(solution)/shard_map/ppermute | solution.py:41
  163.6 17.8 %collective-permute-start.16 = (bf16[768,384]{1,0:T(8,128)(2,1)}, bf16[768,384]{1,0:T(8,128)(2,1)}, u32[]{:S(2)}, u32[]{:S(2)}) collective-permute-start(bf16[768,384]{1,0:T(8,128)(2,1)} %slice.72), channel_id=1, source_target_pairs={{0,192},{64,0},{128,64},{192,128},{1,193},{65,1},{129,65},{193,129... | collective-permute-start | bytes 1769480 | tf_op jit(solution)/shard_map/ppermute | solution.py:41
  200.2 15.1 %copy-start.18 = (bf16[1536,384]{1,0:T(8,128)(2,1)S(1)}, bf16[1536,384]{1,0:T(8,128)(2,1)}, u32[]{:S(2)}) copy-start(bf16[1536,384]{1,0:T(8,128)(2,1)} %get-tuple-element.27) | copy-start | bytes 3538948
  200.2 50.0 %all-to-all-start.2 = ((bf16[64,24,512]{2,1,0:T(8,128)(2,1)}), bf16[64,24,512]{2,1,0:T(8,128)(2,1)}, u32[]{:S(2)}, u32[]{:S(2)}) async-start(bf16[64,24,512]{2,1,0:T(8,128)(2,1)} %bitcast.73), calls=%async_computation.2 | async-start | bytes 3145728 | tf_op jit(solution)/shard_map/all_to_all | solution.py:369
  210.8 16.9 %copy-start.19 = (bf16[1536,384]{1,0:T(8,128)(2,1)S(1)}, bf16[1536,384]{1,0:T(8,128)(2,1)}, u32[]{:S(2)}) copy-start(bf16[1536,384]{1,0:T(8,128)(2,1)} %get-tuple-element.25) | copy-start | bytes 3538948
  210.9 16.9 %collective-permute-start.17 = (bf16[768,384]{1,0:T(8,128)(2,1)}, bf16[768,384]{1,0:T(8,128)(2,1)S(1)}, u32[]{:S(2)}, u32[]{:S(2)}) collective-permute-start(bf16[768,384]{1,0:T(8,128)(2,1)} %get-tuple-element.26), channel_id=1, source_target_pairs={{0,64},{64,128},{128,192},{192,0},{1,65},{65,129},{129,193},{193,1... | collective-permute-start | bytes 1769480 | tf_op jit(solution)/shard_map/ppermute | solution.py:41
  210.9 18.1 %collective-permute-start.19 = (bf16[768,384]{1,0:T(8,128)(2,1)}, bf16[768,384]{1,0:T(8,128)(2,1)S(1)}, u32[]{:S(2)}, u32[]{:S(2)}) collective-permute-start(bf16[768,384]{1,0:T(8,128)(2,1)} %get-tuple-element.28), channel_id=1, source_target_pairs={{0,192},{64,0},{128,64},{192,128},{1,193},{65,1},{129,65},{193,129... | collective-permute-start | bytes 1769480 | tf_op jit(solution)/shard_map/ppermute | solution.py:41
  229.1 28.8 %collective-permute-start.18 = (bf16[1536,384]{1,0:T(8,128)(2,1)}, bf16[1536,384]{1,0:T(8,128)(2,1)}, u32[]{:S(2)}, u32[]{:S(2)}) collective-permute-start(bf16[1536,384]{1,0:T(8,128)(2,1)} %pad_maximum_fusion.1), channel_id=1, source_target_pairs={{0,64},{64,128},{128,192},{192,0},{1,65},{65,129},{129,193},{193,1... | collective-permute-start | bytes 3538952 | tf_op jit(solution)/shard_map/ppermute | solution.py:41
  230.5 28.8 %collective-permute-start.20 = (bf16[1536,384]{1,0:T(8,128)(2,1)}, bf16[1536,384]{1,0:T(8,128)(2,1)}, u32[]{:S(2)}, u32[]{:S(2)}) collective-permute-start(bf16[1536,384]{1,0:T(8,128)(2,1)} %pad_maximum_fusion.2), channel_id=1, source_target_pairs={{0,192},{64,0},{128,64},{192,128},{1,193},{65,1},{129,65},{193,129... | collective-permute-start | bytes 3538952 | tf_op jit(solution)/shard_map/ppermute | solution.py:41
  252.8 9.8 %all-to-all-start.3 = ((bf16[4,128,128]{2,1,0:T(8,128)(2,1)}), bf16[4,128,128]{2,1,0:T(8,128)(2,1)S(1)}, u32[]{:S(2)}, u32[]{:S(2)}) async-start(bf16[4,128,128]{2,1,0:T(8,128)(2,1)} %weigh.1), calls=%async_computation.3 | async-start | bytes 262144 | tf_op jit(solution)/shard_map/all_to_all | solution.py:397
  262.7 42.0 %copy-start.13 = (bf16[128,512]{1,0:T(8,128)(2,1)S(1)}, bf16[128,512]{1,0:T(8,128)(2,1)}, u32[]{:S(2)}) copy-start(bf16[128,512]{1,0:T(8,128)(2,1)} %copy-done.12) | copy-start | bytes 393220
  (16 other events, 22.7 us)
where the time goes:
time: 308 us; the launch traced here: 306 us
  waiting for transfers between devices  109 us (35%)
  starting transfers between devices  64.2 us (21%)
  blocking collectives  53.1 us (17%)
  Pallas kernels  38.7 us (13%)
  local copies, waits for them, and re-layouts  14.7 us (5%)
  other arithmetic  13.6 us (4%)
  matrix products  11.8 us (4%)
    ppermute x17, waiting for transfers between devices, shift(): lax.ppermute(value, axis, [(i, (i + step) % count) for i in range(count)])  75.6 us
    all_to_all x1, blocking collectives, exchange(): lax.all_to_all(wide, ('dp', 'expert'), split_axis=0, concat_axis=0, tiled...  42 us
    all_to_all x3, waiting for transfers between devices, exchange(): lax.all_to_all(wide, ('dp', 'expert'), split_axis=0, concat_axis=0, tiled...  33.9 us
    all_to_all x3, starting transfers between devices, exchange(): lax.all_to_all(wide, ('dp', 'expert'), split_axis=0, concat_axis=0, tiled...  32.9 us
    ppermute x17, starting transfers between devices, shift(): lax.ppermute(value, axis, [(i, (i + step) % count) for i in range(count)])  27.4 us
    pallas_call x1, Pallas kernels, hidden_units(): pl.pallas_call(functools.partial(hidden_body, columns, sections), out_sha...  11.6 us
    all_gather x1, blocking collectives, per_device(): late_all = lax.all_gather(late, 'section', axis=1, tiled=True)  11.1 us
    unnamed x46, local copies, waits for them, and re-layouts  10.7 us
  transfers between devices with their start and end apart: 25, of which 12 were waited for; matrix products, arithmetic and copies ran while one was open for 5% of the time, Pallas kernels for 4%

commit v1 on v0

v1 whole, which is shorter than its diff:
```python
import functools
import math

import jax
import jax.numpy as jnp
from jax import lax
from jax.experimental import pallas as pl
from jax.experimental.pallas import tpu as pltpu
from jax.sharding import PartitionSpec as P


D_VIT = 1152
HEADS = 16
TOP = 6
BF = jnp.bfloat16
F32 = jnp.float32

LATE = 128
VMEM = pl.BlockSpec(memory_space=pltpu.VMEM)
SMEM = pl.BlockSpec(memory_space=pltpu.SMEM)


def params(mib):
    return pltpu.CompilerParams(vmem_limit_bytes=mib * 2**20)


def dot(a, b):
    return jnp.dot(a, b, preferred_element_type=F32)


def dot_tn(a, b):
    return lax.dot_general(a, b, (((0,), (0,)), ((), ())), preferred_element_type=F32)


def dot_nt(a, b):
    return lax.dot_general(a, b, (((1,), (1,)), ((), ())), preferred_element_type=F32)


def shift(value, axis, step):
    count = lax.axis_size(axis)
    return lax.ppermute(value, axis, [(i, (i + step) % count) for i in range(count)])


def partner(value):
    count = lax.axis_size("dp")
    return lax.ppermute(value, "dp", [(i, i ^ 1) for i in range(count)])


def route_tables(routes, gates, expert_total, capacity):
    rows = routes.shape[0]
    ids = jnp.arange(expert_total, dtype=jnp.int32)
    named = routes[:, :, None] == ids[None, None, :]
    member = jnp.any(named, axis=1)
    weight = jnp.sum(jnp.where(named, gates[:, :, None], 0.0), axis=1)
    places = jnp.arange(rows, dtype=jnp.int32)
    before = (places[:, None] > places[None, :]).astype(BF)
    slot = dot(before, member.astype(BF))
    slot = jnp.where(member, slot, 255.0).astype(BF)
    lanes = jnp.arange(expert_total * capacity, dtype=jnp.int32)
    spread = (lanes[None, :] // capacity == ids[:, None]).astype(BF)
    hit = dot(slot, spread) == (lanes % capacity).astype(F32)[None, :]
    pick = dot_tn(spread, slot.T) == (lanes % capacity).astype(F32)[:, None]
    high = weight.astype(BF)
    low = (weight - high.astype(F32)).astype(BF)
    gate_high = jnp.where(hit, dot(high, spread), 0.0).astype(BF)
    gate_low = jnp.where(hit, dot(low, spread), 0.0).astype(BF)
    return pick.astype(BF), jnp.concatenate([gate_high, gate_low], axis=0)


def hbm(shape, dtype):
    return pltpu.MemorySpace.HBM(shape, dtype)


def keep(*values):
    return [pltpu.with_memory_space_constraint(v, pltpu.MemorySpace.HBM) for v in values]


def attend_body(head_dim, ends, patches, w, out, qkv, bias, heads):
    rows = patches.shape[0]
    values = patches[...].astype(F32)
    center = values - jnp.mean(values, axis=-1, keepdims=True)
    spread = jnp.mean(center * center, axis=-1, keepdims=True)
    normed = (center * lax.rsqrt(spread + 1e-06)).astype(BF)
    qkv[...] = dot_nt(w[...], normed)
    images = ends.shape[0]

    def image_of(axis):
        place = lax.broadcasted_iota(jnp.int32, (rows, 1) if axis == 0 else (1, rows), axis)
        return sum((place >= ends[i]).astype(jnp.int32) for i in range(images))

    bias[...] = jnp.where(image_of(0) == image_of(1), 0.0, -1e30)

    def one(h, carry):
        base = pl.multiple_of(h * 3 * head_dim, 8)
        query = (qkv[pl.ds(base, head_dim), :] * (1.0 / math.sqrt(head_dim))).astype(BF)
        key = qkv[pl.ds(base + head_dim, head_dim), :].astype(BF)
        value = qkv[pl.ds(base + 2 * head_dim, head_dim), :].astype(BF)
        scores = dot_tn(key, query) + bias[...]
        weights = jnp.exp(scores - jnp.max(scores, axis=0, keepdims=True))
        total = jnp.sum(weights, axis=0, keepdims=True)
        heads[pl.ds(pl.multiple_of(h * head_dim, 8), head_dim), :] = dot(value, weights.astype(BF)) / total
        return carry

    lax.fori_loop(0, w.shape[0] // (3 * head_dim), one, 0)
    out[...] = heads[...].astype(BF)


def attend(head_dim, ends, patches, w):
    rows = patches.shape[0]
    features = w.shape[0]
    return pl.pallas_call(
        functools.partial(attend_body, head_dim),
        out_shape=hbm((features // 3, rows), BF),
        in_specs=[SMEM, VMEM, VMEM],
        out_specs=VMEM,
        scratch_shapes=[
            pltpu.VMEM((features, rows), F32),
            pltpu.VMEM((rows, rows), F32),
            pltpu.VMEM((features // 3, rows), F32),
        ],
        compiler_params=params(24),
        name="attend",
    )(ends, patches, w)


def project_body(place, patches, *refs):
    att, w_out, out_rows, out_other, rows, pick = refs[0:4], refs[4], refs[5:8], refs[8], refs[9:17], refs[17]
    own_out, late_out, slot_out = refs[18:21]
    att_v, out_v, proj_v, enc, sems = refs[21:]
    row_y, core = place[0], place[1]
    half = rows[0].shape[0]
    copies = []
    for d in range(4):
        copies.append(pltpu.make_async_copy(att[d], att_v.at[d], sems.at[d]))
    copies.append(pltpu.make_async_copy(w_out, out_v.at[0], sems.at[4]))
    part = out_rows[0].shape[0]
    for d in (1, 2, 3):
        mine = pl.multiple_of(core * part, 16)
        other = pl.multiple_of((1 - core) * part, 16)
        copies.append(pltpu.make_async_copy(out_rows[d - 1], out_v.at[d, pl.ds(mine, part)], sems.at[4 + d]))
        copies.append(
            pltpu.make_async_copy(out_other.at[pl.ds((d - 1) * part, part)], out_v.at[d, pl.ds(other, part)], sems.at[15 + d])
        )
    first = len(copies)
    for d in range(4):
        mine = pl.multiple_of(core * half, 64)
        other = pl.multiple_of((1 - core) * half, 64)
        copies.append(pltpu.make_async_copy(rows[d], proj_v.at[d, pl.ds(mine, half)], sems.at[8 + d]))
        copies.append(pltpu.make_async_copy(rows[4 + d], proj_v.at[d, pl.ds(other, half)], sems.at[12 + d]))
    for c in copies:
        c.start()
    for c in copies[:first]:
        c.wait()
    step = 128
    for r in range(patches.shape[0] // step):
        at = pl.ds(r * step, step)
        total = patches[at, :].astype(F32)
        for d in range(4):
            total += dot_tn(att_v[d, :, at], out_v[d])
        for q in range(enc.shape[0]):
            enc[q, at, :] = total[:, q * 128 : (q + 1) * 128]
    for c in copies[first:]:
        c.wait()
    merged = patches.shape[0] // 4
    acc = jnp.zeros(own_out.shape, F32)
    for d in range(4):
        j = lax.rem(row_y + 4 - d, 4)
        block = [enc[q, pl.ds(j, merged, stride=4), :].astype(BF) for q in range(enc.shape[0])]
        acc += dot(jnp.concatenate(block, axis=1), proj_v[d])
    own = acc.astype(BF)
    own_out[...] = own
    early = slot_out.shape[1]
    late_out[...] = own[:, early:]
    slot_out[...] = dot(pick[...], own[:, :early]).astype(BF)


def project(place, patches, att, w_out, out_rows, out_other, proj_rows, pick):
    merged = patches.shape[0] // 4
    columns = proj_rows[0].shape[1]
    half = proj_rows[0].shape[0]
    slots = pick.shape[0]
    anyspace = pl.BlockSpec(memory_space=pl.ANY)
    return pl.pallas_call(
        project_body,
        out_shape=(
            hbm((merged, columns), BF),
            jax.ShapeDtypeStruct((merged, LATE), BF),
            hbm((slots, columns - LATE), BF),
        ),
        in_specs=[SMEM, VMEM] + [anyspace] * 17 + [VMEM],
        out_specs=(VMEM, VMEM, VMEM),
        scratch_shapes=[
            pltpu.VMEM((4,) + att[0].shape, BF),
            pltpu.VMEM((4,) + w_out.shape, BF),
            pltpu.VMEM((4, 2 * half, columns), BF),
            pltpu.VMEM((patches.shape[1] // 128, patches.shape[0], 128), F32),
            pltpu.SemaphoreType.DMA((19,)),
        ],
        compiler_params=params(24),
        name="project",
    )(place, patches, *att, w_out, *out_rows, out_other, *proj_rows, pick)


def pick_body(pick, late, out):
    out[...] = dot(pick[...], late[...]).astype(BF)


def pick_rows(pick, late):
    return pl.pallas_call(
        pick_body,
        out_shape=hbm((pick.shape[0], late.shape[1]), BF),
        compiler_params=params(8),
        name="pick_rows",
    )(pick, late)


def squares(x):
    wide = x.astype(F32)
    wide = wide * wide
    return sum(wide[:, q * 128 : (q + 1) * 128] for q in range(x.shape[1] // 128))


ROWS = 384


def rows_spec(width, index=lambda r, *place: (r, 0)):
    return pl.BlockSpec((ROWS, width), index)


def lane_block(height, width, offset, sections):
    return pl.BlockSpec(
        (height, width), lambda r, place: (0, lax.rem(place[0] + offset, sections)), pipeline_mode=pl.Buffered(1)
    )


def whole_block(shape):
    return pl.BlockSpec(shape, lambda r, place: (0, 0), pipeline_mode=pl.Buffered(1))


def over_rows(body, rows, in_specs, out_specs, out_shape, operands):
    return pl.pallas_call(
        body,
        grid_spec=pltpu.PrefetchScalarGridSpec(
            num_scalar_prefetch=1, grid=(rows // ROWS,), in_specs=in_specs, out_specs=out_specs
        ),
        out_shape=out_shape,
        compiler_params=params(20),
    )(*operands)


def up_body(place, own, left, right, w_own, w_left, w_right, acc_out, square_out):
    width = own.shape[1]
    acc = jnp.zeros(acc_out.shape, F32)
    square = jnp.zeros(square_out.shape, F32)
    for piece, w in ((own, w_own), (left, w_left), (right, w_right)):
        x = piece[...]
        acc += dot_nt(x, w[:, :width])
        square += squares(x)
    acc_out[...] = acc
    square_out[...] = square


def up(columns, sections, place, own, left, right, w):
    rows, width = own.shape
    count = w.shape[0]
    return over_rows(
        up_body,
        rows,
        [rows_spec(width)] * 3 + [lane_block(count, columns, o, sections) for o in (0, 3, 1)],
        (rows_spec(count), rows_spec(128)),
        (hbm((rows, count), F32), hbm((rows, 128), F32)),
        (place, *keep(own, left, right, w, w, w)),
    )


def hidden_body(full, place, acc, square, late, far_a, far_b, w, w_late, w_down, hid_out, to_a, to_b):
    hidden_count = w_down.shape[0]
    width = far_a.shape[1]
    in_a = pl.program_id(0) < pl.num_programs(0) // 2
    x = jnp.where(in_a, far_a[...], far_b[...])
    y = late[...]
    total = acc[...] + dot_nt(x, w[:, :width])
    total += dot_nt(y, w_late[...])
    square_sum = square[...] + squares(x) + squares(y)
    mean = jnp.sum(square_sum, axis=-1, keepdims=True) * (1.0 / full)
    row_scale = lax.rsqrt(mean + 1e-06)
    gate = total[:, :hidden_count] * row_scale
    upper = total[:, hidden_count:] * row_scale
    hidden = (gate / (1.0 + jnp.exp(-gate)) * upper).astype(BF)
    hid_out[...] = hidden
    part = dot(hidden, w_down[:, :width]).astype(BF)

    @pl.when(in_a)
    def _():
        to_a[...] = part

    @pl.when(jnp.logical_not(in_a))
    def _():
        to_b[...] = part


def hidden_units(columns, sections, place, acc, square, late, far_a, far_b, w, w_late, w_down):
    rows, width = acc.shape[0], far_a.shape[1]
    half = rows // 2 // ROWS
    spec_a = rows_spec(width, lambda r, place: (jnp.minimum(r, half - 1), 0))
    spec_b = rows_spec(width, lambda r, place: (jnp.maximum(r - half, 0), 0))
    return over_rows(
        functools.partial(hidden_body, columns * sections),
        rows,
        [rows_spec(acc.shape[1]), rows_spec(128), rows_spec(late.shape[1]), spec_a, spec_b]
        + [lane_block(w.shape[0], columns, 2, sections), whole_block(w_late.shape)]
        + [lane_block(w_down.shape[0], columns, 2, sections)],
        (rows_spec(w_down.shape[0]), spec_a, spec_b),
        (hbm((rows, w_down.shape[0]), BF), hbm((rows // 2, width), BF), hbm((rows // 2, width), BF)),
        (place, *keep(acc, square, late, far_a, far_b, w, w_late, w_down)),
    )


def down_body(count, place, hidden, *refs):
    h = hidden[...]
    for w, out in zip(refs[:count], refs[count:]):
        out[...] = dot(h, w[:, : out.shape[1]]).astype(BF)


def down(columns, sections, offsets, place, hidden, w, width):
    rows, height = hidden.shape
    count = len(offsets) or 1
    blocks = [lane_block(height, columns, o, sections) for o in offsets] or [whole_block(w.shape)]
    return over_rows(
        functools.partial(down_body, count),
        rows,
        [rows_spec(height)] + blocks,
        [rows_spec(width)] * count,
        [hbm((rows, width), BF)] * count,
        (place, *keep(hidden, *[w] * count)),
    )


def cut_body(left, right, top, bottom):
    top[...] = left[...]
    bottom[...] = right[...]


def cut(left, right):
    rows, width = left.shape
    half = rows // 2 // ROWS
    return pl.pallas_call(
        cut_body,
        out_shape=(hbm((rows // 2, width), BF),) * 2,
        grid=(half,),
        in_specs=[rows_spec(width), rows_spec(width, lambda r: (r + half, 0))],
        out_specs=[rows_spec(width)] * 2,
        compiler_params=params(8),
        name="cut",
    )(*keep(left, right))


def add_body(right, left, via_a, via_b, right_out, left_out):
    right_out[...] = (right[...].astype(F32) + via_a[...].astype(F32)).astype(BF)
    left_out[...] = (left[...].astype(F32) + via_b[...].astype(F32)).astype(BF)


def add(right, left, via_a, via_b):
    rows, width = right.shape
    half = rows // 2 // ROWS
    whole = [rows_spec(width), rows_spec(width, lambda r: (r + half, 0))]
    return pl.pallas_call(
        add_body,
        out_shape=(hbm(right.shape, BF), hbm(left.shape, BF)),
        grid=(half,),
        in_specs=whole + [rows_spec(width)] * 2,
        out_specs=whole,
        input_output_aliases={0: 0, 1: 1},
        compiler_params=params(8),
        name="add",
    )(*keep(right, left, via_a, via_b))


def weigh_body(gates, late, out):
    both = dot(gates[...], late[...])
    merged = both.shape[0] // 2
    out[...] = (both[:merged] + both[merged:]).astype(BF)


def weigh(gates, late):
    return pl.pallas_call(
        weigh_body,
        out_shape=jax.ShapeDtypeStruct((gates.shape[0] // 2, late.shape[1]), BF),
        compiler_params=params(12),
        name="weigh",
    )(gates, late)


def combine_body(sections, place, gates, own, late, early, out):
    merged, _ = own.shape
    width = early.shape[1]
    both = dot(gates[...], early[...])
    out[:, :width] = (own[:, :width].astype(F32) + both[:merged] + both[merged:]).astype(BF)
    total = own[:, width:].astype(F32)
    for s in range(sections):
        first = s * sections * LATE + place[0] * LATE
        total += late[:, pl.ds(pl.multiple_of(first, LATE), LATE)].astype(F32)
    out[:, width:] = total.astype(BF)


def combine(sections, place, gates, own, late, early):
    return pl.pallas_call(
        functools.partial(combine_body, sections),
        out_shape=jax.ShapeDtypeStruct(own.shape, BF),
        in_specs=[SMEM] + [VMEM] * 4,
        out_specs=VMEM,
        compiler_params=params(12),
        name="combine",
    )(place, *keep(gates, own, late), early)


def per_device(patches, lengths, w_qkv, w_out, w_proj, routes, gates, w_gate, w_up, w_down):
    data_count = lax.axis_size("dp")
    owner_count = lax.axis_size("expert")
    sections = lax.axis_size("section")
    merged_count = patches.shape[0] // 4
    expert_total = data_count * owner_count
    capacity = max(2, min(merged_count, 2 * merged_count * TOP // expert_total))
    columns = w_proj.shape[1]
    early = columns - LATE
    place = jnp.stack([lax.axis_index("section")]).astype(jnp.int32)
    dp_place = jnp.stack([lax.axis_index("dp") // 2, lax.axis_index("dp") % 2]).astype(jnp.int32)

    out_rows, mine = [], [w_proj]
    out_half = lax.dynamic_slice_in_dim(w_out, dp_place[1] * (w_out.shape[0] // 2), w_out.shape[0] // 2, axis=0)
    for d in (1, 2, 3):
        mine.append(shift(w_proj, "dp", 2 * d))
        out_rows.append(shift(out_half, "section", d))
    proj_rows = mine + [partner(m) for m in mine]
    out_other = partner(jnp.concatenate(out_rows, axis=0))

    ends = jnp.cumsum(lengths[0]).astype(jnp.int32) * 4
    attended = attend(D_VIT // HEADS, ends, patches, w_qkv.T)

    att = [attended]
    for d in (1, 2, 3):
        att.append(shift(attended, "section", d))
    pick, gate_rows = route_tables(routes, gates, expert_total, capacity)
    w_both = jnp.concatenate([w_gate[0].T, w_up[0].T], axis=0)
    last = lambda w: jnp.concatenate([w[:, s * columns + early : (s + 1) * columns] for s in range(sections)], axis=1)
    w_late, down_late = last(w_both), last(w_down[0])
    proj_own, late, outgoing = project(dp_place, patches, att, w_out, out_rows, out_other, proj_rows, pick)

    def exchange(value):
        wide = value.reshape(expert_total, capacity, value.shape[1])
        wide = lax.all_to_all(wide, ("dp", "expert"), split_axis=0, concat_axis=0, tiled=True)
        return wide.reshape(value.shape)

    own = exchange(outgoing)
    late_all = lax.all_gather(late, "section", axis=1, tiled=True)
    late_rows = pick_rows(pick, late_all)
    late_rows = exchange(late_rows)
    left = shift(own, "section", 1)
    right = shift(own, "section", -1)
    top, bottom = cut(left, right)
    far_a = shift(top, "section", 1)
    far_b = shift(bottom, "section", -1)
    acc, square = up(columns, sections, place, own, left, right, w_both)
    hidden, to_a, to_b = hidden_units(
        columns, sections, place, acc, square, late_rows, far_a, far_b, w_both, w_late, w_down[0]
    )
    via_a = shift(to_a, "section", 1)
    via_b = shift(to_b, "section", -1)
    (late_out,) = down(columns, sections, (), place, hidden, down_late, LATE * sections)
    late_back = exchange(late_out)
    to_right, to_left, here = down(columns, sections, (1, 3, 0), place, hidden, w_down[0], early)
    to_right, to_left = add(to_right, to_left, via_a, via_b)
    from_left = shift(to_right, "section", 1)
    from_right = shift(to_left, "section", -1)
    total = (here.astype(F32) + from_left.astype(F32) + from_right.astype(F32)).astype(BF)
    returned = exchange(total)
    late_sum = weigh(gate_rows, late_back)
    late_sum = lax.all_gather(late_sum, "section", axis=1, tiled=True)
    return combine(sections, place, gate_rows, proj_own, late_sum, returned)


def solution(mesh):
    return jax.shard_map(
        per_device,
        mesh=mesh,
        in_specs=(
            P(("dp", "expert"), None),
            P(("dp", "expert"), None),
            P(None, "section"),
            P("section", None),
            P("dp", "section"),
            P(("dp", "expert"), None),
            P(("dp", "expert"), None),
            P(("dp", "expert"), None, "section"),
            P(("dp", "expert"), None, "section"),
            P(("dp", "expert"), "section", None),
        ),
        out_specs=P(("dp", "expert"), "section"),
        check_vma=False,
    )
```

time: 308 us -> 286 us (0.929)
  blocking collectives: 53.1 us -> 24.4 us
  Pallas kernels: 38.7 us -> 50.8 us
  matrix products: 11.8 us -> 1.52 us
  waiting for transfers between devices: 109 us -> 116 us
  other arithmetic: 13.6 us -> 8.26 us
    all_to_all x1 -> x0, blocking collectives: 42 us -> none  [exchange(): lax.all_to_all(wide, ('dp', 'expert'), split_axis=0, concat_axis=0, tiled...]
    all_gather x0 -> x1, blocking collectives: none -> 13.5 us  [per_device(): late_sum = lax.all_gather(late_sum, 'section', axis=1, tiled=True)]
    pallas_call x7 -> x11, Pallas kernels: 38.7 us -> 50.8 us  [the longest x4 27.2 us: over_rows(): pl.pallas_call(body, grid_spec=pltpu.PrefetchScalarGridSpec(num_scalar_pr...]
    all_to_all x3 -> x4, starting transfers between devices: 32.9 us -> 39.7 us  [exchange(): lax.all_to_all(wide, ('dp', 'expert'), split_axis=0, concat_axis=0, tiled...]
    sub x1 -> x0, matrix products: 4.98 us -> none  [per_device(): weights = jnp.where(same[None], jnp.exp(scores - peak), 0.0)]
    ppermute x17, waiting for transfers between devices: 75.6 us -> 80.3 us  [shift(): lax.ppermute(value, axis, [(i, (i + step) % count) for i in range(count)])]
    all_to_all x1 -> x0, starting transfers between devices: 3.32 us -> none  [per_device(): lax.all_to_all(late_sum, 'section', split_axis=0, concat_axis=0, tiled=True)]
    unnamed x46 -> x58, local copies, waits for them, and re-layouts: 10.7 us -> 13.5 us
  transfers between devices with their start and end apart: 25 -> 26, of which waited for: 12 -> 10; matrix products, arithmetic and copies ran while one was open for 5% -> 4% of each run, Pallas kernels for 4% -> 9%
where the time goes in v1:
time: 286 us; the launch traced here: 284 us
  waiting for transfers between devices  116 us (41%)
  starting transfers between devices  65.7 us (23%)
  Pallas kernels  50.8 us (18%)
  blocking collectives  24.4 us (9%)
  local copies, waits for them, and re-layouts  16.3 us (6%)
  other arithmetic  8.26 us (3%)
    ppermute x17, waiting for transfers between devices, shift(): lax.ppermute(value, axis, [(i, (i + step) % count) for i in range(count)])  80.3 us
    all_to_all x4, starting transfers between devices, exchange(): lax.all_to_all(wide, ('dp', 'expert'), split_axis=0, concat_axis=0, tiled...  39.7 us
    all_to_all x4, waiting for transfers between devices, exchange(): lax.all_to_all(wide, ('dp', 'expert'), split_axis=0, concat_axis=0, tiled...  34.6 us
    pallas_call x4, Pallas kernels, over_rows(): pl.pallas_call(body, grid_spec=pltpu.PrefetchScalarGridSpec(num_scalar_pr...  27.2 us
    ppermute x17, starting transfers between devices, shift(): lax.ppermute(value, axis, [(i, (i + step) % count) for i in range(count)])  25.4 us
    all_gather x1, blocking collectives, per_device(): late_sum = lax.all_gather(late_sum, 'section', axis=1, tiled=True)  13.5 us
    unnamed x58, local copies, waits for them, and re-layouts  13.5 us
    all_gather x1, blocking collectives, per_device(): late_all = lax.all_gather(late, 'section', axis=1, tiled=True)  10.9 us
  transfers between devices with their start and end apart: 26, of which 10 were waited for; matrix products, arithmetic and copies ran while one was open for 4% of the time, Pallas kernels for 9%

profile of v1, /device:TPU:8, one launch (start us, length us, event | category | flops | bytes accessed | tf_op | source)
XLA Modules:
  0.0 283.6 jit_solution(4221770176746703420)
XLA Ops:
  0.0 1.7 constant_dynamic-slice_fusion
  3.2 2.7 collective-permute-start.4
  11.1 6.1 %attend.1.refs_0_ = bf16[288,512]{1,0:T(8,128)(2,1)} custom-call(s32[4]{0:T(128)S(1)} %multiply_bitcast_fusion.ends, bf16[512,1152]{1,0:T(8,128)(2,1)S(1)} %copy-done.1, bf16[864,1152]{1,0:T(8,128)(2,1)S(1)} %bitcast.27), custom_call_target="tpu_custom_call" | custom-call | tf_op jit(solution)/shard_map/attend/pallas_call | solution.py:111
  21.9 2.3 collective-permute-start.8
  26.6 7.1 %collective-permute-done.refs_1_ = bf16[288,512]{1,0:T(8,128)(2,1)S(1)} collective-permute-done((bf16[288,512]{1,0:T(8,128)(2,1)}, bf16[288,512]{1,0:T(8,128)(2,1)S(1)}, u32[]{:S(2)}, u32[]{:S(2)}) %collective-permute-start) | collective-permute-done | bytes 294944 | tf_op jit(solution)/shard_map/ppermute | solution.py:41
  35.2 9.6 %collective-permute-done.2.refs_3_ = bf16[288,512]{1,0:T(8,128)(2,1)S(1)} collective-permute-done((bf16[288,512]{1,0:T(8,128)(2,1)}, bf16[288,512]{1,0:T(8,128)(2,1)S(1)}, u32[]{:S(2)}, u32[]{:S(2)}) %collective-permute-start.2) | collective-permute-done | bytes 294944 | tf_op jit(solution)/shard_map/ppermute | solution.py:41
  46.1 3.3 %collective-permute-done.9.refs_12_ = bf16[576,512]{1,0:T(8,128)(2,1)} collective-permute-done((bf16[576,512]{1,0:T(8,128)(2,1)}, bf16[576,512]{1,0:T(8,128)(2,1)}, u32[]{:S(2)}, u32[]{:S(2)}) %collective-permute-start.9) | collective-permute-done | bytes 589856 | tf_op jit(solution)/shard_map/ppermute | solution.py:41
  54.6 7.9 %project.1 = (bf16[128,512]{1,0:T(8,128)(2,1)}, bf16[128,128]{1,0:T(8,128)(2,1)S(1)}, bf16[1536,384]{1,0:T(8,128)(2,1)}) custom-call(s32[2]{0:T(128)S(1)} %pad_add_fusion.place, bf16[512,1152]{1,0:T(8,128)(2,1)S(1)} %copy-done.2, bf16[288,512]{1,0:T(8,128)(2,1)S(1)} %copy-done.5, bf16[288,512]{1,0:T(8,128)(2,1)S(1)} %copy-done.7, ...), custom_call_target="tpu_custom_call" | custom-call | tf_op jit(solution)/shard_map/project/pallas_call | solution.py:183
  63.1 12.2 %all-to-all-start = ((bf16[64,24,384]{2,1,0:T(8,128)(2,1)}), bf16[64,24,384]{2,1,0:T(8,128)(2,1)}, u32[]{:S(2)}, u32[]{:S(2)}) async-start(bf16[64,24,384]{2,1,0:T(8,128)(2,1)} %bitcast.41), calls=%async_computation | async-start | bytes 2359296 | tf_op jit(solution)/shard_map/all_to_all | solution.py:451
  75.4 10.9 %all_gather.6.late = bf16[128,512]{1,0:T(8,128)(2,1)S(1)} all-gather(bf16[128,128]{1,0:T(8,128)(2,1)S(1)} %copy-done.13), channel_id=1, replica_groups=mesh['section'=4,'dp'=8,'expert'=8] {'section'}, dimensions={1}, use_global_device_ids=true | all-gather | bytes 163840 | tf_op jit(solution)/shard_map/all_gather | solution.py:455
  86.2 1.7 pick_rows.1
  88.0 18.5 %all-to-all-done = bf16[64,24,384]{2,1,0:T(8,128)(2,1)} async-done(((bf16[64,24,384]{2,1,0:T(8,128)(2,1)}), bf16[64,24,384]{2,1,0:T(8,128)(2,1)}, u32[]{:S(2)}, u32[]{:S(2)}) %all-to-all-start) | async-done | bytes 1179680 | tf_op jit(solution)/shard_map/all_to_all | solution.py:451
  106.5 6.5 %all-to-all-start.1 = ((bf16[64,24,512]{2,1,0:T(8,128)(2,1)}), bf16[64,24,512]{2,1,0:T(8,128)(2,1)S(1)}, u32[]{:S(2)}, u32[]{:S(2)}) async-start(bf16[64,24,512]{2,1,0:T(8,128)(2,1)} %bitcast.34), calls=%async_computation.1 | async-start | bytes 3145728 | tf_op jit(solution)/shard_map/all_to_all | solution.py:451
  113.5 2.8 collective-permute-start.15
  117.4 25.1 %collective-permute-done.14.left = bf16[1536,384]{1,0:T(8,128)(2,1)S(1)} collective-permute-done((bf16[1536,384]{1,0:T(8,128)(2,1)}, bf16[1536,384]{1,0:T(8,128)(2,1)S(1)}, u32[]{:S(2)}, u32[]{:S(2)}) %collective-permute-start.14) | collective-permute-done | bytes 1179680 | tf_op jit(solution)/shard_map/ppermute | solution.py:41
  144.6 2.1 cut.1
  146.8 3.2 %collective-permute-start.17 = (bf16[768,384]{1,0:T(8,128)(2,1)}, bf16[768,384]{1,0:T(8,128)(2,1)}, u32[]{:S(2)}, u32[]{:S(2)}) collective-permute-start(bf16[768,384]{1,0:T(8,128)(2,1)} %get-tuple-element.26), channel_id=1, source_target_pairs={{0,192},{64,0},{128,64},{192,128},{1,193},{65,1},{129,65},{193,129... | collective-permute-start | bytes 1769480 | tf_op jit(solution)/shard_map/ppermute | solution.py:41
  153.5 1.9 pad_maximum_fusion.w_own.w_left.w_right.w
  155.4 8.0 %shard_map.100 = (f32[1536,704]{1,0:T(8,128)}, f32[1536,128]{1,0:T(8,128)}) custom-call(s32[1]{0:T(128)} %bitcast.place, bf16[1536,384]{1,0:T(8,128)(2,1)} %bitcast.7.own, bf16[1536,384]{1,0:T(8,128)(2,1)} %copy-done.17, bf16[1536,384]{1,0:T(8,128)(2,1)} %copy-done.18, bf16[704,2048]{1,0:T(8,128)(2,1)} %pad_maximum_fusion.w_own.w_left.w_right.w, ...), custom_call_target="tpu_custom_call" | custom-call | tf_op jit(solution)/shard_map/pallas_call | solution.py:241
  164.5 9.7 %shard_map.101 = (bf16[1536,352]{1,0:T(8,128)(2,1)}, bf16[768,384]{1,0:T(8,128)(2,1)}, bf16[768,384]{1,0:T(8,128)(2,1)}) custom-call(s32[1]{0:T(128)} %bitcast.place, f32[1536,704]{1,0:T(8,128)} %get-tuple-element.22.acc, f32[1536,128]{1,0:T(8,128)} %get-tuple-element.23.square, bf16[1536,512]{1,0:T(8,128)(2,1)} %bitcast.33, ...), custom_call_target="tpu_custom_call" | custom-call | tf_op jit(solution)/shard_map/pallas_call | solution.py:241
  174.2 4.3 %shard_map.102 = bf16[1536,512]{1,0:T(8,128)(2,1)} custom-call(s32[1]{0:T(128)} %bitcast.place, bf16[1536,352]{1,0:T(8,128)(2,1)} %get-tuple-element.27.hidden, bf16[352,512]{1,0:T(8,128)(2,1)} %pad_maximum_fusion.4.refs_0_), custom_call_target="tpu_custom_call" | custom-call | tf_op jit(solution)/shard_map/pallas_call | solution.py:241
  178.5 10.4 %all-to-all-start.2 = ((bf16[64,24,512]{2,1,0:T(8,128)(2,1)}), bf16[64,24,512]{2,1,0:T(8,128)(2,1)S(1)}, u32[]{:S(2)}, u32[]{:S(2)}) async-start(bf16[64,24,512]{2,1,0:T(8,128)(2,1)} %bitcast.35), calls=%async_computation.2 | async-start | bytes 3145728 | tf_op jit(solution)/shard_map/all_to_all | solution.py:451
  189.1 3.2 %collective-permute-start.19 = (bf16[768,384]{1,0:T(8,128)(2,1)S(1)}, bf16[768,384]{1,0:T(8,128)(2,1)S(1)}, u32[]{:S(2)}, u32[]{:S(2)}) collective-permute-start(bf16[768,384]{1,0:T(8,128)(2,1)S(1)} %copy-done.27), channel_id=1, source_target_pairs={{0,192},{64,0},{128,64},{192,128},{1,193},{65,1},{129,65},{193,129... | collective-permute-start | bytes 1769480 | tf_op jit(solution)/shard_map/ppermute | solution.py:41
  192.3 5.3 %shard_map.103 = (bf16[1536,384]{1,0:T(8,128)(2,1)}, bf16[1536,384]{1,0:T(8,128)(2,1)}, bf16[1536,384]{1,0:T(8,128)(2,1)}) custom-call(s32[1]{0:T(128)} %bitcast.place, bf16[1536,352]{1,0:T(8,128)(2,1)} %get-tuple-element.27.hidden, bf16[352,2048]{1,0:T(8,128)(2,1)} %bitcast.30, bf16[352,2048]{1,0:T(8,128)(2,1)} %bitcast.31, bf16[352,2048]{1,0:T(8,128)(2,1)} %bitcast.32), custom_call_target="tpu_custom_call" | custom-call | tf_op jit(solution)/shard_map/pallas_call | solution.py:241
  197.6 8.0 %collective-permute-done.18.via_a = bf16[768,384]{1,0:T(8,128)(2,1)S(1)} collective-permute-done((bf16[768,384]{1,0:T(8,128)(2,1)S(1)}, bf16[768,384]{1,0:T(8,128)(2,1)S(1)}, u32[]{:S(2)}, u32[]{:S(2)}) %collective-permute-start.18) | collective-permute-done | bytes 589856 | tf_op jit(solution)/shard_map/ppermute | solution.py:41
  206.7 2.6 add.53
  209.3 3.2 %collective-permute-start.21 = (bf16[1536,384]{1,0:T(8,128)(2,1)}, bf16[1536,384]{1,0:T(8,128)(2,1)S(1)}, u32[]{:S(2)}, u32[]{:S(2)}) collective-permute-start(bf16[1536,384]{1,0:T(8,128)(2,1)} %get-tuple-element.34), channel_id=1, source_target_pairs={{0,192},{64,0},{128,64},{192,128},{1,193},{65,1},{129,65},{193,129... | collective-permute-start | bytes 3538952 | tf_op jit(solution)/shard_map/ppermute | solution.py:41
  212.5 25.4 %collective-permute-done.20 = bf16[1536,384]{1,0:T(8,128)(2,1)S(1)} collective-permute-done((bf16[1536,384]{1,0:T(8,128)(2,1)}, bf16[1536,384]{1,0:T(8,128)(2,1)S(1)}, u32[]{:S(2)}, u32[]{:S(2)}) %collective-permute-start.20) | collective-permute-done | bytes 1179680 | tf_op jit(solution)/shard_map/ppermute | solution.py:41
  239.4 10.5 %all-to-all-start.3 = ((bf16[64,24,384]{2,1,0:T(8,128)(2,1)}), bf16[64,24,384]{2,1,0:T(8,128)(2,1)S(1)}, u32[]{:S(2)}, u32[]{:S(2)}) async-start(bf16[64,24,384]{2,1,0:T(8,128)(2,1)} %bitcast.40), calls=%async_computation.3 | async-start | bytes 2359296 | tf_op jit(solution)/shard_map/all_to_all | solution.py:451
  251.4 13.5 %all_gather.7.late = bf16[128,2048]{1,0:T(8,128)(2,1)} all-gather(bf16[128,512]{1,0:T(8,128)(2,1)S(1)} %weigh.1), channel_id=1, replica_groups=mesh['section'=4,'dp'=8,'expert'=8] {'section'}, dimensions={1}, use_global_device_ids=true | all-gather | bytes 655360 | tf_op jit(solution)/shard_map/all_gather | solution.py:478
  265.0 16.1 %all-to-all-done.3 = bf16[64,24,384]{2,1,0:T(8,128)(2,1)S(1)} async-done(((bf16[64,24,384]{2,1,0:T(8,128)(2,1)}), bf16[64,24,384]{2,1,0:T(8,128)(2,1)S(1)}, u32[]{:S(2)}, u32[]{:S(2)}) %all-to-all-start.3) | async-done | bytes 1179680 | tf_op jit(solution)/shard_map/all_to_all | solution.py:451
  281.1 2.6 combine.1
  (111 shorter events, 34.8 us)
Async XLA Ops:
  1.7 16.9 %collective-permute-start.3 = (bf16[144,1152]{1,0:T(8,128)(2,1)}, bf16[144,1152]{1,0:T(8,128)(2,1)S(1)}, u32[]{:S(2)}, u32[]{:S(2)}) collective-permute-start(bf16[144,1152]{1,0:T(8,128)(2,1)} %constant_dynamic-slice_fusion), channel_id=1, source_target_pairs={{0,64},{64,128},{128,192},{192,0},{1,65},{65,129},{129,193},{193,1... | collective-permute-start | bytes 995336 | tf_op jit(solution)/shard_map/ppermute | solution.py:41
  3.2 18.7 %collective-permute-start.4 = (bf16[144,1152]{1,0:T(8,128)(2,1)}, bf16[144,1152]{1,0:T(8,128)(2,1)S(1)}, u32[]{:S(2)}, u32[]{:S(2)}) collective-permute-start(bf16[144,1152]{1,0:T(8,128)(2,1)} %constant_dynamic-slice_fusion), channel_id=1, source_target_pairs={{0,128},{64,192},{128,0},{192,64},{1,129},{65,193},{129,1},{193,65... | collective-permute-start | bytes 995336 | tf_op jit(solution)/shard_map/ppermute | solution.py:41
  6.0 18.3 %collective-permute-start.5 = (bf16[144,1152]{1,0:T(8,128)(2,1)}, bf16[144,1152]{1,0:T(8,128)(2,1)S(1)}, u32[]{:S(2)}, u32[]{:S(2)}) collective-permute-start(bf16[144,1152]{1,0:T(8,128)(2,1)} %constant_dynamic-slice_fusion), channel_id=1, source_target_pairs={{0,192},{64,0},{128,64},{192,128},{1,193},{65,1},{129,65},{193,129... | collective-permute-start | bytes 995336 | tf_op jit(solution)/shard_map/ppermute | solution.py:41
  11.1 38.5 %copy-start.22 = (s32[128,6]{0,1:T(8,128)S(1)}, s32[128,6]{0,1:T(8,128)}, u32[]{:S(2)}) copy-start(s32[128,6]{0,1:T(8,128)} %param.15) | copy-start | bytes 9220
  17.2 34.5 %copy-start.2 = (bf16[512,1152]{1,0:T(8,128)(2,1)S(1)}, bf16[512,1152]{1,0:T(8,128)(2,1)}, u32[]{:S(2)}) copy-start(bf16[512,1152]{1,0:T(8,128)(2,1)} %patches.3) | copy-start | bytes 3538948
  17.2 34.5 %copy-start.4 = (bf16[288,1152]{1,0:T(8,128)(2,1)S(1)}, bf16[288,1152]{1,0:T(8,128)(2,1)}, u32[]{:S(2)}) copy-start(bf16[288,1152]{1,0:T(8,128)(2,1)} %refs_4_.1) | copy-start | bytes 1990660
  17.2 34.5 %copy-start.5 = (bf16[288,512]{1,0:T(8,128)(2,1)S(1)}, bf16[288,512]{1,0:T(8,128)(2,1)}, u32[]{:S(2)}) copy-start(bf16[288,512]{1,0:T(8,128)(2,1)} %attend.1.refs_0_) | copy-start | bytes 884740
  17.2 16.5 %collective-permute-start = (bf16[288,512]{1,0:T(8,128)(2,1)}, bf16[288,512]{1,0:T(8,128)(2,1)S(1)}, u32[]{:S(2)}, u32[]{:S(2)}) collective-permute-start(bf16[288,512]{1,0:T(8,128)(2,1)} %attend.1.refs_0_), channel_id=1, source_target_pairs={{0,64},{64,128},{128,192},{192,0},{1,65},{65,129},{129,193},{193,1... | collective-permute-start | bytes 884744 | tf_op jit(solution)/shard_map/ppermute | solution.py:41
  17.7 16.7 %collective-permute-start.1 = (bf16[288,512]{1,0:T(8,128)(2,1)}, bf16[288,512]{1,0:T(8,128)(2,1)S(1)}, u32[]{:S(2)}, u32[]{:S(2)}) collective-permute-start(bf16[288,512]{1,0:T(8,128)(2,1)} %attend.1.refs_0_), channel_id=1, source_target_pairs={{0,128},{64,192},{128,0},{192,64},{1,129},{65,193},{129,1},{193,65... | collective-permute-start | bytes 884744 | tf_op jit(solution)/shard_map/ppermute | solution.py:41
  18.6 26.9 %collective-permute-start.7 = (bf16[576,512]{1,0:T(8,128)(2,1)}, bf16[576,512]{1,0:T(8,128)(2,1)}, u32[]{:S(2)}, u32[]{:S(2)}) collective-permute-start(bf16[576,512]{1,0:T(8,128)(2,1)} %refs_9_.1), channel_id=1, source_target_pairs={{0,16},{8,24},{16,32},{24,40},{32,48},{40,56},{48,0},{56,8},{1,17}... | collective-permute-start | bytes 1769480 | tf_op jit(solution)/shard_map/ppermute | solution.py:41
  21.9 24.1 %collective-permute-start.8 = (bf16[576,512]{1,0:T(8,128)(2,1)}, bf16[576,512]{1,0:T(8,128)(2,1)}, u32[]{:S(2)}, u32[]{:S(2)}) collective-permute-start(bf16[576,512]{1,0:T(8,128)(2,1)} %refs_9_.1), channel_id=1, source_target_pairs={{0,32},{8,40},{16,48},{24,56},{32,0},{40,8},{48,16},{56,24},{1,33}... | collective-permute-start | bytes 1769480 | tf_op jit(solution)/shard_map/ppermute | solution.py:41
  24.2 25.2 %collective-permute-start.9 = (bf16[576,512]{1,0:T(8,128)(2,1)}, bf16[576,512]{1,0:T(8,128)(2,1)}, u32[]{:S(2)}, u32[]{:S(2)}) collective-permute-start(bf16[576,512]{1,0:T(8,128)(2,1)} %refs_9_.1), channel_id=1, source_target_pairs={{0,48},{8,56},{16,0},{24,8},{32,16},{40,24},{48,32},{56,40},{1,49}... | collective-permute-start | bytes 1769480 | tf_op jit(solution)/shard_map/ppermute | solution.py:41
  34.4 17.3 %collective-permute-start.6 = (bf16[432,1152]{1,0:T(8,128)(2,1)}, bf16[432,1152]{1,0:T(8,128)(2,1)}, u32[]{:S(2)}, u32[]{:S(2)}) collective-permute-start(bf16[432,1152]{1,0:T(8,128)(2,1)} %pad_maximum_fusion.1), channel_id=1, source_target_pairs={{0,8},{8,0},{16,24},{24,16},{32,40},{40,32},{48,56},{56,48},{1,9},... | collective-permute-start | bytes 2985992 | tf_op jit(solution)/shard_map/ppermute | solution.py:46
  35.2 9.6 %collective-permute-start.2 = (bf16[288,512]{1,0:T(8,128)(2,1)}, bf16[288,512]{1,0:T(8,128)(2,1)S(1)}, u32[]{:S(2)}, u32[]{:S(2)}) collective-permute-start(bf16[288,512]{1,0:T(8,128)(2,1)} %attend.1.refs_0_), channel_id=1, source_target_pairs={{0,192},{64,0},{128,64},{192,128},{1,193},{65,1},{129,65},{193,129... | collective-permute-start | bytes 884744 | tf_op jit(solution)/shard_map/ppermute | solution.py:41
  45.5 4.7 %collective-permute-start.10 = (bf16[576,512]{1,0:T(8,128)(2,1)}, bf16[576,512]{1,0:T(8,128)(2,1)S(1)}, u32[]{:S(2)}, u32[]{:S(2)}) collective-permute-start(bf16[576,512]{1,0:T(8,128)(2,1)} %refs_9_.1), channel_id=1, source_target_pairs={{0,8},{8,0},{16,24},{24,16},{32,40},{40,32},{48,56},{56,48},{1,9},... | collective-permute-start | bytes 1769480 | tf_op jit(solution)/shard_map/ppermute | solution.py:46
  45.5 4.7 %collective-permute-start.11 = (bf16[576,512]{1,0:T(8,128)(2,1)}, bf16[576,512]{1,0:T(8,128)(2,1)S(1)}, u32[]{:S(2)}, u32[]{:S(2)}) collective-permute-start(bf16[576,512]{1,0:T(8,128)(2,1)} %collective-permute-done.7.refs_10_), channel_id=1, source_target_pairs={{0,8},{8,0},{16,24},{24,16},{32,40},{40,32},{48,56},{56,48},{1,9},... | collective-permute-start | bytes 1769480 | tf_op jit(solution)/shard_map/ppermute | solution.py:46
  46.0 4.2 %collective-permute-start.12 = (bf16[576,512]{1,0:T(8,128)(2,1)}, bf16[576,512]{1,0:T(8,128)(2,1)S(1)}, u32[]{:S(2)}, u32[]{:S(2)}) collective-permute-start(bf16[576,512]{1,0:T(8,128)(2,1)} %collective-permute-done.8.refs_11_), channel_id=1, source_target_pairs={{0,8},{8,0},{16,24},{24,16},{32,40},{40,32},{48,56},{56,48},{1,9},... | collective-permute-start | bytes 1769480 | tf_op jit(solution)/shard_map/ppermute | solution.py:46
  49.5 2.2 collective-permute-start.13
  63.1 43.4 %all-to-all-start = ((bf16[64,24,384]{2,1,0:T(8,128)(2,1)}), bf16[64,24,384]{2,1,0:T(8,128)(2,1)}, u32[]{:S(2)}, u32[]{:S(2)}) async-start(bf16[64,24,384]{2,1,0:T(8,128)(2,1)} %bitcast.41), calls=%async_computation | async-start | bytes 2359296 | tf_op jit(solution)/shard_map/all_to_all | solution.py:451
  106.5 56.8 %all-to-all-start.1 = ((bf16[64,24,512]{2,1,0:T(8,128)(2,1)}), bf16[64,24,512]{2,1,0:T(8,128)(2,1)S(1)}, u32[]{:S(2)}, u32[]{:S(2)}) async-start(bf16[64,24,512]{2,1,0:T(8,128)(2,1)} %bitcast.34), calls=%async_computation.1 | async-start | bytes 3145728 | tf_op jit(solution)/shard_map/all_to_all | solution.py:451
  113.0 29.5 %collective-permute-start.14 = (bf16[1536,384]{1,0:T(8,128)(2,1)}, bf16[1536,384]{1,0:T(8,128)(2,1)S(1)}, u32[]{:S(2)}, u32[]{:S(2)}) collective-permute-start(bf16[1536,384]{1,0:T(8,128)(2,1)} %bitcast.7.own), channel_id=1, source_target_pairs={{0,64},{64,128},{128,192},{192,0},{1,65},{65,129},{129,193},{193,1... | collective-permute-start | bytes 3538952 | tf_op jit(solution)/shard_map/ppermute | solution.py:41
  113.5 29.0 %collective-permute-start.15 = (bf16[1536,384]{1,0:T(8,128)(2,1)}, bf16[1536,384]{1,0:T(8,128)(2,1)S(1)}, u32[]{:S(2)}, u32[]{:S(2)}) collective-permute-start(bf16[1536,384]{1,0:T(8,128)(2,1)} %bitcast.7.own), channel_id=1, source_target_pairs={{0,192},{64,0},{128,64},{192,128},{1,193},{65,1},{129,65},{193,129... | collective-permute-start | bytes 3538952 | tf_op jit(solution)/shard_map/ppermute | solution.py:41
  117.4 33.4 %copy-start.15 = (bf16[1,2048,352]{1,2,0:T(8,128)(2,1)S(1)}, bf16[1,2048,352]{1,2,0:T(8,128)(2,1)}, u32[]{:S(2)}) copy-start(bf16[1,2048,352]{1,2,0:T(8,128)(2,1)} %param.18) | copy-start | bytes 4325380
  146.8 16.6 %collective-permute-start.16 = (bf16[768,384]{1,0:T(8,128)(2,1)}, bf16[768,384]{1,0:T(8,128)(2,1)}, u32[]{:S(2)}, u32[]{:S(2)}) collective-permute-start(bf16[768,384]{1,0:T(8,128)(2,1)} %get-tuple-element.25), channel_id=1, source_target_pairs={{0,64},{64,128},{128,192},{192,0},{1,65},{65,129},{129,193},{193,1... | collective-permute-start | bytes 1769480 | tf_op jit(solution)/shard_map/ppermute | solution.py:41
  146.8 16.6 %collective-permute-start.17 = (bf16[768,384]{1,0:T(8,128)(2,1)}, bf16[768,384]{1,0:T(8,128)(2,1)}, u32[]{:S(2)}, u32[]{:S(2)}) collective-permute-start(bf16[768,384]{1,0:T(8,128)(2,1)} %get-tuple-element.26), channel_id=1, source_target_pairs={{0,192},{64,0},{128,64},{192,128},{1,193},{65,1},{129,65},{193,129... | collective-permute-start | bytes 1769480 | tf_op jit(solution)/shard_map/ppermute | solution.py:41
  178.5 60.8 %all-to-all-start.2 = ((bf16[64,24,512]{2,1,0:T(8,128)(2,1)}), bf16[64,24,512]{2,1,0:T(8,128)(2,1)S(1)}, u32[]{:S(2)}, u32[]{:S(2)}) async-start(bf16[64,24,512]{2,1,0:T(8,128)(2,1)} %bitcast.35), calls=%async_computation.2 | async-start | bytes 3145728 | tf_op jit(solution)/shard_map/all_to_all | solution.py:451
  189.0 16.7 %collective-permute-start.18 = (bf16[768,384]{1,0:T(8,128)(2,1)S(1)}, bf16[768,384]{1,0:T(8,128)(2,1)S(1)}, u32[]{:S(2)}, u32[]{:S(2)}) collective-permute-start(bf16[768,384]{1,0:T(8,128)(2,1)S(1)} %copy-done.28), channel_id=1, source_target_pairs={{0,64},{64,128},{128,192},{192,0},{1,65},{65,129},{129,193},{193,1... | collective-permute-start | bytes 1769480 | tf_op jit(solution)/shard_map/ppermute | solution.py:41
  189.1 16.6 %collective-permute-start.19 = (bf16[768,384]{1,0:T(8,128)(2,1)S(1)}, bf16[768,384]{1,0:T(8,128)(2,1)S(1)}, u32[]{:S(2)}, u32[]{:S(2)}) collective-permute-start(bf16[768,384]{1,0:T(8,128)(2,1)S(1)} %copy-done.27), channel_id=1, source_target_pairs={{0,192},{64,0},{128,64},{192,128},{1,193},{65,1},{129,65},{193,129... | collective-permute-start | bytes 1769480 | tf_op jit(solution)/shard_map/ppermute | solution.py:41
  206.7 31.2 %copy-start.19 = (bf16[1536,384]{1,0:T(8,128)(2,1)S(1)}, bf16[1536,384]{1,0:T(8,128)(2,1)}, u32[]{:S(2)}) copy-start(bf16[1536,384]{1,0:T(8,128)(2,1)} %get-tuple-element.28) | copy-start | bytes 3538948
  209.3 28.6 %collective-permute-start.20 = (bf16[1536,384]{1,0:T(8,128)(2,1)}, bf16[1536,384]{1,0:T(8,128)(2,1)S(1)}, u32[]{:S(2)}, u32[]{:S(2)}) collective-permute-start(bf16[1536,384]{1,0:T(8,128)(2,1)} %get-tuple-element.33), channel_id=1, source_target_pairs={{0,64},{64,128},{128,192},{192,0},{1,65},{65,129},{129,193},{193,1... | collective-permute-start | bytes 3538952 | tf_op jit(solution)/shard_map/ppermute | solution.py:41
  209.3 28.6 %collective-permute-start.21 = (bf16[1536,384]{1,0:T(8,128)(2,1)}, bf16[1536,384]{1,0:T(8,128)(2,1)S(1)}, u32[]{:S(2)}, u32[]{:S(2)}) collective-permute-start(bf16[1536,384]{1,0:T(8,128)(2,1)} %get-tuple-element.34), channel_id=1, source_target_pairs={{0,192},{64,0},{128,64},{192,128},{1,193},{65,1},{129,65},{193,129... | collective-permute-start | bytes 3538952 | tf_op jit(solution)/shard_map/ppermute | solution.py:41
  239.4 41.7 %all-to-all-start.3 = ((bf16[64,24,384]{2,1,0:T(8,128)(2,1)}), bf16[64,24,384]{2,1,0:T(8,128)(2,1)S(1)}, u32[]{:S(2)}, u32[]{:S(2)}) async-start(bf16[64,24,384]{2,1,0:T(8,128)(2,1)} %bitcast.40), calls=%async_computation.3 | async-start | bytes 2359296 | tf_op jit(solution)/shard_map/all_to_all | solution.py:451
  (23 other events, 96.2 us)

commit v2 on v1

--- a/solution.py
+++ b/solution.py
@@ -75,20 +75,29 @@
     return [pltpu.with_memory_space_constraint(v, pltpu.MemorySpace.HBM) for v in values]
 
 
-def attend_body(head_dim, ends, patches, w, out, qkv, bias, heads):
+def attend_body(head_dim, lengths, patches_hbm, w_hbm, out, patches, w, qkv, bias, heads, sems):
     rows = patches.shape[0]
+    get_patches = pltpu.make_async_copy(patches_hbm, patches, sems.at[0])
+    get_w = pltpu.make_async_copy(w_hbm, w, sems.at[1])
+    get_patches.start()
+    get_w.start()
+    ends, end = [], 0
+    for i in range(lengths.shape[1]):
+        end = end + lengths[0, i] * 4
+        ends.append(end)
+
+    def image_of(axis):
+        place = lax.broadcasted_iota(jnp.int32, (rows, 1) if axis == 0 else (1, rows), axis)
+        return sum((place >= end).astype(jnp.int32) for end in ends)
+
+    bias[...] = jnp.where(image_of(0) == image_of(1), 0.0, -1e30)
+    get_patches.wait()
     values = patches[...].astype(F32)
     center = values - jnp.mean(values, axis=-1, keepdims=True)
     spread = jnp.mean(center * center, axis=-1, keepdims=True)
-    normed = (center * lax.rsqrt(spread + 1e-06)).astype(BF)
-    qkv[...] = dot_nt(w[...], normed)
-    images = ends.shape[0]
-
-    def image_of(axis):
-        place = lax.broadcasted_iota(jnp.int32, (rows, 1) if axis == 0 else (1, rows), axis)
-        return sum((place >= ends[i]).astype(jnp.int32) for i in range(images))
-
-    bias[...] = jnp.where(image_of(0) == image_of(1), 0.0, -1e30)
+    patches[...] = (center * lax.rsqrt(spread + 1e-06)).astype(BF)
+    get_w.wait()
+    qkv[...] = dot_nt(w[...], patches[...])
 
     def one(h, carry):
         base = pl.multiple_of(h * 3 * head_dim, 8)
@@ -101,26 +110,29 @@
         heads[pl.ds(pl.multiple_of(h * head_dim, 8), head_dim), :] = dot(value, weights.astype(BF)) / total
         return carry
 
-    lax.fori_loop(0, w.shape[0] // (3 * head_dim), one, 0)
+    lax.fori_loop(0, w.shape[0] // (3 * head_dim), one, 0, unroll=4)
     out[...] = heads[...].astype(BF)
 
 
-def attend(head_dim, ends, patches, w):
+def attend(head_dim, lengths, patches, w):
     rows = patches.shape[0]
     features = w.shape[0]
     return pl.pallas_call(
         functools.partial(attend_body, head_dim),
         out_shape=hbm((features // 3, rows), BF),
-        in_specs=[SMEM, VMEM, VMEM],
+        in_specs=[SMEM, pl.BlockSpec(memory_space=pl.ANY), pl.BlockSpec(memory_space=pl.ANY)],
         out_specs=VMEM,
         scratch_shapes=[
+            pltpu.VMEM(patches.shape, BF),
+            pltpu.VMEM(w.shape, BF),
             pltpu.VMEM((features, rows), F32),
             pltpu.VMEM((rows, rows), F32),
             pltpu.VMEM((features // 3, rows), F32),
+            pltpu.SemaphoreType.DMA((2,)),
         ],
         compiler_params=params(24),
         name="attend",
-    )(ends, patches, w)
+    )(*keep(lengths, patches, w))
 
 
 def project_body(place, patches, *refs):
@@ -130,16 +142,17 @@
     row_y, core = place[0], place[1]
     half = rows[0].shape[0]
     copies = []
+    height = w_out.shape[0]
     for d in range(4):
-        copies.append(pltpu.make_async_copy(att[d], att_v.at[d], sems.at[d]))
-    copies.append(pltpu.make_async_copy(w_out, out_v.at[0], sems.at[4]))
+        copies.append(pltpu.make_async_copy(att[d], att_v.at[pl.ds(d * height, height)], sems.at[d]))
+    copies.append(pltpu.make_async_copy(w_out, out_v.at[pl.ds(0, height)], sems.at[4]))
     part = out_rows[0].shape[0]
     for d in (1, 2, 3):
-        mine = pl.multiple_of(core * part, 16)
-        other = pl.multiple_of((1 - core) * part, 16)
-        copies.append(pltpu.make_async_copy(out_rows[d - 1], out_v.at[d, pl.ds(mine, part)], sems.at[4 + d]))
+        mine = pl.multiple_of(d * height + core * part, 16)
+        other = pl.multiple_of(d * height + (1 - core) * part, 16)
+        copies.append(pltpu.make_async_copy(out_rows[d - 1], out_v.at[pl.ds(mine, part)], sems.at[4 + d]))
         copies.append(
-            pltpu.make_async_copy(out_other.at[pl.ds((d - 1) * part, part)], out_v.at[d, pl.ds(other, part)], sems.at[15 + d])
+            pltpu.make_async_copy(out_other.at[pl.ds((d - 1) * part, part)], out_v.at[pl.ds(other, part)], sems.at[15 + d])
         )
     first = len(copies)
     for d in range(4):
@@ -154,9 +167,7 @@
     step = 128
     for r in range(patches.shape[0] // step):
         at = pl.ds(r * step, step)
-        total = patches[at, :].astype(F32)
-        for d in range(4):
-            total += dot_tn(att_v[d, :, at], out_v[d])
+        total = patches[at, :].astype(F32) + dot_tn(att_v[:, at], out_v[...])
         for q in range(enc.shape[0]):
             enc[q, at, :] = total[:, q * 128 : (q + 1) * 128]
     for c in copies[first:]:
@@ -190,8 +201,8 @@
         in_specs=[SMEM, VMEM] + [anyspace] * 17 + [VMEM],
         out_specs=(VMEM, VMEM, VMEM),
         scratch_shapes=[
-            pltpu.VMEM((4,) + att[0].shape, BF),
-            pltpu.VMEM((4,) + w_out.shape, BF),
+            pltpu.VMEM((4 * att[0].shape[0], att[0].shape[1]), BF),
+            pltpu.VMEM((4 * w_out.shape[0], w_out.shape[1]), BF),
             pltpu.VMEM((4, 2 * half, columns), BF),
             pltpu.VMEM((patches.shape[1] // 128, patches.shape[0], 128), F32),
             pltpu.SemaphoreType.DMA((19,)),
@@ -273,7 +284,8 @@
     )
 
 
-def hidden_body(full, place, acc, square, late, far_a, far_b, w, w_late, w_down, hid_out, to_a, to_b):
+def hidden_body(full, place, acc, square, late, far_a, far_b, w, w_late, w_down, down_late, *outs):
+    hid_out, to_a, to_b, late_out = outs
     hidden_count = w_down.shape[0]
     width = far_a.shape[1]
     in_a = pl.program_id(0) < pl.num_programs(0) // 2
@@ -288,6 +300,7 @@
     upper = total[:, hidden_count:] * row_scale
     hidden = (gate / (1.0 + jnp.exp(-gate)) * upper).astype(BF)
     hid_out[...] = hidden
+    late_out[...] = dot(hidden, down_late[...]).astype(BF)
     part = dot(hidden, w_down[:, :width]).astype(BF)
 
     @pl.when(in_a)
@@ -299,7 +312,7 @@
         to_b[...] = part
 
 
-def hidden_units(columns, sections, place, acc, square, late, far_a, far_b, w, w_late, w_down):
+def hidden_units(columns, sections, place, acc, square, late, far_a, far_b, w, w_late, w_down, down_late):
     rows, width = acc.shape[0], far_a.shape[1]
     half = rows // 2 // ROWS
     spec_a = rows_spec(width, lambda r, place: (jnp.minimum(r, half - 1), 0))
@@ -309,10 +322,10 @@
         rows,
         [rows_spec(acc.shape[1]), rows_spec(128), rows_spec(late.shape[1]), spec_a, spec_b]
         + [lane_block(w.shape[0], columns, 2, sections), whole_block(w_late.shape)]
-        + [lane_block(w_down.shape[0], columns, 2, sections)],
-        (rows_spec(w_down.shape[0]), spec_a, spec_b),
-        (hbm((rows, w_down.shape[0]), BF), hbm((rows // 2, width), BF), hbm((rows // 2, width), BF)),
-        (place, *keep(acc, square, late, far_a, far_b, w, w_late, w_down)),
+        + [lane_block(w_down.shape[0], columns, 2, sections), whole_block(down_late.shape)],
+        (rows_spec(w_down.shape[0]), spec_a, spec_b, rows_spec(late.shape[1])),
+        (hbm((rows, w_down.shape[0]), BF), *[hbm((rows // 2, width), BF)] * 2, hbm(late.shape, BF)),
+        (place, *keep(acc, square), late, *keep(far_a, far_b, w, w_late, w_down, down_late)),
     )
 
 
@@ -324,8 +337,8 @@
 
 def down(columns, sections, offsets, place, hidden, w, width):
     rows, height = hidden.shape
-    count = len(offsets) or 1
-    blocks = [lane_block(height, columns, o, sections) for o in offsets] or [whole_block(w.shape)]
+    count = len(offsets)
+    blocks = [lane_block(height, columns, o, sections) for o in offsets]
     return over_rows(
         functools.partial(down_body, count),
         rows,
@@ -373,7 +386,7 @@
         input_output_aliases={0: 0, 1: 1},
         compiler_params=params(8),
         name="add",
-    )(*keep(right, left, via_a, via_b))
+    )(*keep(right, left), via_a, via_b)
 
 
 def weigh_body(gates, late, out):
@@ -391,27 +404,41 @@
     )(gates, late)
 
 
-def combine_body(sections, place, gates, own, late, early, out):
-    merged, _ = own.shape
-    width = early.shape[1]
-    both = dot(gates[...], early[...])
-    out[:, :width] = (own[:, :width].astype(F32) + both[:merged] + both[merged:]).astype(BF)
+def settle_body(sections, place, own, late, out):
+    width = own.shape[1] - LATE
+    out[:, :width] = own[:, :width].astype(F32)
     total = own[:, width:].astype(F32)
     for s in range(sections):
         first = s * sections * LATE + place[0] * LATE
         total += late[:, pl.ds(pl.multiple_of(first, LATE), LATE)].astype(F32)
-    out[:, width:] = total.astype(BF)
-
-
-def combine(sections, place, gates, own, late, early):
-    return pl.pallas_call(
-        functools.partial(combine_body, sections),
-        out_shape=jax.ShapeDtypeStruct(own.shape, BF),
-        in_specs=[SMEM] + [VMEM] * 4,
+    out[:, width:] = total
+
+
+def settle(sections, place, own, late):
+    return pl.pallas_call(
+        functools.partial(settle_body, sections),
+        out_shape=jax.ShapeDtypeStruct(own.shape, F32),
+        in_specs=[SMEM, VMEM, VMEM],
         out_specs=VMEM,
         compiler_params=params(12),
+        name="settle",
+    )(place, own, late)
+
+
+def combine_body(gates, early, base, out):
+    merged, width = out.shape[0], early.shape[1]
+    both = dot(gates[...], early[...])
+    out[:, :width] = (base[:, :width] + both[:merged] + both[merged:]).astype(BF)
+    out[:, width:] = base[:, width:].astype(BF)
+
+
+def combine(gates, early, base):
+    return pl.pallas_call(
+        combine_body,
+        out_shape=jax.ShapeDtypeStruct(base.shape, BF),
+        compiler_params=params(12),
         name="combine",
-    )(place, *keep(gates, own, late), early)
+    )(gates, early, base)
 
 
 def per_device(patches, lengths, w_qkv, w_out, w_proj, routes, gates, w_gate, w_up, w_down):
@@ -434,8 +461,7 @@
     proj_rows = mine + [partner(m) for m in mine]
     out_other = partner(jnp.concatenate(out_rows, axis=0))
 
-    ends = jnp.cumsum(lengths[0]).astype(jnp.int32) * 4
-    attended = attend(D_VIT // HEADS, ends, patches, w_qkv.T)
+    attended = attend(D_VIT // HEADS, lengths, patches, w_qkv.T)
 
     att = [attended]
     for d in (1, 2, 3):
@@ -461,12 +487,11 @@
     far_a = shift(top, "section", 1)
     far_b = shift(bottom, "section", -1)
     acc, square = up(columns, sections, place, own, left, right, w_both)
-    hidden, to_a, to_b = hidden_units(
-        columns, sections, place, acc, square, late_rows, far_a, far_b, w_both, w_late, w_down[0]
+    hidden, to_a, to_b, late_out = hidden_units(
+        columns, sections, place, acc, square, late_rows, far_a, far_b, w_both, w_late, w_down[0], down_late
     )
     via_a = shift(to_a, "section", 1)
     via_b = shift(to_b, "section", -1)
-    (late_out,) = down(columns, sections, (), place, hidden, down_late, LATE * sections)
     late_back = exchange(late_out)
     to_right, to_left, here = down(columns, sections, (1, 3, 0), place, hidden, w_down[0], early)
     to_right, to_left = add(to_right, to_left, via_a, via_b)
@@ -476,7 +501,8 @@
     returned = exchange(total)
     late_sum = weigh(gate_rows, late_back)
     late_sum = lax.all_gather(late_sum, "section", axis=1, tiled=True)
-    return combine(sections, place, gate_rows, proj_own, late_sum, returned)
+    base = settle(sections, place, proj_own, late_sum)
+    return combine(gate_rows, returned, base)
 
 
 def solution(mesh):

time: 286 us -> 276 us (0.965)
  local copies, waits for them, and re-layouts: 16.3 us -> 10.5 us
  Pallas kernels: 50.8 us -> 45.2 us
  waiting for transfers between devices: 116 us -> 120 us
    unnamed x58 -> x46, local copies, waits for them, and re-layouts: 13.5 us -> 8.47 us
    pallas_call x4 -> x3, Pallas kernels: 27.2 us -> 23.6 us  [over_rows(): pl.pallas_call(body, grid_spec=pltpu.PrefetchScalarGridSpec(num_scalar_pr...]
  transfers between devices with their start and end apart: 26 -> 26, of which waited for: 10 -> 11; matrix products, arithmetic and copies ran while one was open for 4% -> 4% of each run, Pallas kernels for 9% -> 10%
where the time goes in v2:
time: 276 us; the launch traced here: 274 us
  waiting for transfers between devices  120 us (43%)
  starting transfers between devices  66 us (24%)
  Pallas kernels  45.2 us (16%)
  blocking collectives  23.5 us (9%)
  local copies, waits for them, and re-layouts  10.5 us (4%)
  other arithmetic  7.48 us (3%)
    ppermute x17, waiting for transfers between devices, shift(): lax.ppermute(value, axis, [(i, (i + step) % count) for i in range(count)])  82.9 us
    all_to_all x4, starting transfers between devices, exchange(): lax.all_to_all(wide, ('dp', 'expert'), split_axis=0, concat_axis=0, tiled...  39.6 us
    all_to_all x4, waiting for transfers between devices, exchange(): lax.all_to_all(wide, ('dp', 'expert'), split_axis=0, concat_axis=0, tiled...  35.5 us
    ppermute x17, starting transfers between devices, shift(): lax.ppermute(value, axis, [(i, (i + step) % count) for i in range(count)])  25.6 us
    pallas_call x3, Pallas kernels, over_rows(): pl.pallas_call(body, grid_spec=pltpu.PrefetchScalarGridSpec(num_scalar_pr...  23.6 us
    all_gather x1, blocking collectives, per_device(): late_sum = lax.all_gather(late_sum, 'section', axis=1, tiled=True)  12.8 us
    all_gather x1, blocking collectives, per_device(): late_all = lax.all_gather(late, 'section', axis=1, tiled=True)  10.7 us
    unnamed x46, local copies, waits for them, and re-layouts  8.47 us
  transfers between devices with their start and end apart: 26, of which 11 were waited for; matrix products, arithmetic and copies ran while one was open for 4% of the time, Pallas kernels for 10%

profile of v2, /device:TPU:8, one launch (start us, length us, event | category | flops | bytes accessed | tf_op | source)
XLA Modules:
  0.0 274.4 jit_solution(6687885438102263978)
XLA Ops:
  1.0 1.6 collective-permute-start.3
  2.6 2.7 collective-permute-start.4
  6.7 6.7 %attend.1.refs_0_ = bf16[288,512]{1,0:T(8,128)(2,1)} custom-call(s32[1,4]{1,0:T(1,128)} %lengths.1, bf16[512,1152]{1,0:T(8,128)(2,1)} %patches.1, bf16[864,1152]{1,0:T(8,128)(2,1)} %bitcast.36), custom_call_target="tpu_custom_call" | custom-call | tf_op jit(solution)/shard_map/attend/pallas_call | solution.py:120
  15.0 1.6 collective-permute-start.7
  16.6 4.5 %collective-permute-done.4.refs_6_ = bf16[144,1152]{1,0:T(8,128)(2,1)S(1)} collective-permute-done((bf16[144,1152]{1,0:T(8,128)(2,1)S(1)}, bf16[144,1152]{1,0:T(8,128)(2,1)S(1)}, u32[]{:S(2)}, u32[]{:S(2)}) %collective-permute-start.4) | collective-permute-done | bytes 331808 | tf_op jit(solution)/shard_map/ppermute | solution.py:41
  21.1 2.3 collective-permute-start.8
  28.1 4.6 %collective-permute-done.1.refs_2_ = bf16[288,512]{1,0:T(8,128)(2,1)S(1)} collective-permute-done((bf16[288,512]{1,0:T(8,128)(2,1)}, bf16[288,512]{1,0:T(8,128)(2,1)S(1)}, u32[]{:S(2)}, u32[]{:S(2)}) %collective-permute-start.1) | collective-permute-done | bytes 294944 | tf_op jit(solution)/shard_map/ppermute | solution.py:41
  33.4 8.1 %collective-permute-done.2.refs_3_ = bf16[288,512]{1,0:T(8,128)(2,1)S(1)} collective-permute-done((bf16[288,512]{1,0:T(8,128)(2,1)}, bf16[288,512]{1,0:T(8,128)(2,1)S(1)}, u32[]{:S(2)}, u32[]{:S(2)}) %collective-permute-start.2) | collective-permute-done | bytes 294944 | tf_op jit(solution)/shard_map/ppermute | solution.py:41
  43.0 5.7 %collective-permute-done.9.refs_12_ = bf16[576,512]{1,0:T(8,128)(2,1)} collective-permute-done((bf16[576,512]{1,0:T(8,128)(2,1)}, bf16[576,512]{1,0:T(8,128)(2,1)}, u32[]{:S(2)}, u32[]{:S(2)}) %collective-permute-start.9) | collective-permute-done | bytes 589856 | tf_op jit(solution)/shard_map/ppermute | solution.py:41
  53.8 6.9 %project.1 = (bf16[128,512]{1,0:T(8,128)(2,1)}, bf16[128,128]{1,0:T(8,128)(2,1)S(1)}, bf16[1536,384]{1,0:T(8,128)(2,1)}) custom-call(s32[2]{0:T(128)S(1)} %pad_add_fusion.place, bf16[512,1152]{1,0:T(8,128)(2,1)S(1)} %copy-done, bf16[288,512]{1,0:T(8,128)(2,1)S(1)} %copy-done.2, bf16[288,512]{1,0:T(8,128)(2,1)S(1)} %copy-done.4, ...), custom_call_target="tpu_custom_call" | custom-call | tf_op jit(solution)/shard_map/project/pallas_call | solution.py:194
  61.3 12.2 %all-to-all-start = ((bf16[64,24,384]{2,1,0:T(8,128)(2,1)}), bf16[64,24,384]{2,1,0:T(8,128)(2,1)}, u32[]{:S(2)}, u32[]{:S(2)}) async-start(bf16[64,24,384]{2,1,0:T(8,128)(2,1)} %bitcast.38), calls=%async_computation | async-start | bytes 2359296 | tf_op jit(solution)/shard_map/all_to_all | solution.py:477
  73.6 10.7 %all_gather.6.late = bf16[128,512]{1,0:T(8,128)(2,1)S(1)} all-gather(bf16[128,128]{1,0:T(8,128)(2,1)S(1)} %copy-done.11), channel_id=1, replica_groups=mesh['section'=4,'dp'=8,'expert'=8] {'section'}, dimensions={1}, use_global_device_ids=true | all-gather | bytes 163840 | tf_op jit(solution)/shard_map/all_gather | solution.py:481
  84.3 1.8 pick_rows.1
  86.0 18.7 %all-to-all-done = bf16[64,24,384]{2,1,0:T(8,128)(2,1)} async-done(((bf16[64,24,384]{2,1,0:T(8,128)(2,1)}), bf16[64,24,384]{2,1,0:T(8,128)(2,1)}, u32[]{:S(2)}, u32[]{:S(2)}) %all-to-all-start) | async-done | bytes 1179680 | tf_op jit(solution)/shard_map/all_to_all | solution.py:477
  104.7 6.5 %all-to-all-start.1 = ((bf16[64,24,512]{2,1,0:T(8,128)(2,1)}), bf16[64,24,512]{2,1,0:T(8,128)(2,1)S(1)}, u32[]{:S(2)}, u32[]{:S(2)}) async-start(bf16[64,24,512]{2,1,0:T(8,128)(2,1)} %bitcast.30), calls=%async_computation.1 | async-start | bytes 3145728 | tf_op jit(solution)/shard_map/all_to_all | solution.py:477
  111.3 3.2 %collective-permute-start.15 = (bf16[1536,384]{1,0:T(8,128)(2,1)}, bf16[1536,384]{1,0:T(8,128)(2,1)S(1)}, u32[]{:S(2)}, u32[]{:S(2)}) collective-permute-start(bf16[1536,384]{1,0:T(8,128)(2,1)} %bitcast.5.own), channel_id=1, source_target_pairs={{0,192},{64,0},{128,64},{192,128},{1,193},{65,1},{129,65},{193,129... | collective-permute-start | bytes 3538952 | tf_op jit(solution)/shard_map/ppermute | solution.py:41
  115.6 25.1 %collective-permute-done.14.left = bf16[1536,384]{1,0:T(8,128)(2,1)S(1)} collective-permute-done((bf16[1536,384]{1,0:T(8,128)(2,1)}, bf16[1536,384]{1,0:T(8,128)(2,1)S(1)}, u32[]{:S(2)}, u32[]{:S(2)}) %collective-permute-start.14) | collective-permute-done | bytes 1179680 | tf_op jit(solution)/shard_map/ppermute | solution.py:41
  142.9 2.1 cut.1
  145.0 3.2 %collective-permute-start.17 = (bf16[768,384]{1,0:T(8,128)(2,1)}, bf16[768,384]{1,0:T(8,128)(2,1)}, u32[]{:S(2)}, u32[]{:S(2)}) collective-permute-start(bf16[768,384]{1,0:T(8,128)(2,1)} %get-tuple-element.26), channel_id=1, source_target_pairs={{0,192},{64,0},{128,64},{192,128},{1,193},{65,1},{129,65},{193,129... | collective-permute-start | bytes 1769480 | tf_op jit(solution)/shard_map/ppermute | solution.py:41
  151.7 1.9 pad_maximum_fusion.w_own.w_left.w_right.w
  153.6 8.0 %shard_map.100 = (f32[1536,704]{1,0:T(8,128)}, f32[1536,128]{1,0:T(8,128)}) custom-call(s32[1]{0:T(128)} %bitcast.place, bf16[1536,384]{1,0:T(8,128)(2,1)} %bitcast.5.own, bf16[1536,384]{1,0:T(8,128)(2,1)} %copy-done.14, bf16[1536,384]{1,0:T(8,128)(2,1)} %copy-done.15, bf16[704,2048]{1,0:T(8,128)(2,1)} %pad_maximum_fusion.w_own.w_left.w_right.w, ...), custom_call_target="tpu_custom_call" | custom-call | tf_op jit(solution)/shard_map/pallas_call | solution.py:252
  161.6 10.3 %shard_map.101 = (bf16[1536,352]{1,0:T(8,128)(2,1)}, bf16[768,384]{1,0:T(8,128)(2,1)}, bf16[768,384]{1,0:T(8,128)(2,1)}, bf16[1536,512]{1,0:T(8,128)(2,1)}) custom-call(s32[1]{0:T(128)} %bitcast.place, f32[1536,704]{1,0:T(8,128)} %get-tuple-element.22.acc, f32[1536,128]{1,0:T(8,128)} %get-tuple-element.23.square, bf16[1536,512]{1,0:T(8,128)(2,1)S(1)} %bitcast.23, ...), custom_call_target="tpu_custom_call" | custom-call | tf_op jit(solution)/shard_map/pallas_call | solution.py:252
  171.9 10.5 %all-to-all-start.3 = ((bf16[64,24,512]{2,1,0:T(8,128)(2,1)}), bf16[64,24,512]{2,1,0:T(8,128)(2,1)S(1)}, u32[]{:S(2)}, u32[]{:S(2)}) async-start(bf16[64,24,512]{2,1,0:T(8,128)(2,1)} %bitcast.37), calls=%async_computation.3 | async-start | bytes 3145728 | tf_op jit(solution)/shard_map/all_to_all | solution.py:477
  182.5 3.2 %collective-permute-start.19 = (bf16[768,384]{1,0:T(8,128)(2,1)S(1)}, bf16[768,384]{1,0:T(8,128)(2,1)S(1)}, u32[]{:S(2)}, u32[]{:S(2)}) collective-permute-start(bf16[768,384]{1,0:T(8,128)(2,1)S(1)} %copy-done.21), channel_id=1, source_target_pairs={{0,192},{64,0},{128,64},{192,128},{1,193},{65,1},{129,65},{193,129... | collective-permute-start | bytes 1769480 | tf_op jit(solution)/shard_map/ppermute | solution.py:41
  185.7 5.3 %shard_map.102 = (bf16[1536,384]{1,0:T(8,128)(2,1)}, bf16[1536,384]{1,0:T(8,128)(2,1)}, bf16[1536,384]{1,0:T(8,128)(2,1)}) custom-call(s32[1]{0:T(128)} %bitcast.place, bf16[1536,352]{1,0:T(8,128)(2,1)} %get-tuple-element.27.hidden, bf16[352,2048]{1,0:T(8,128)(2,1)} %bitcast.27, bf16[352,2048]{1,0:T(8,128)(2,1)} %bitcast.28, bf16[352,2048]{1,0:T(8,128)(2,1)} %bitcast.29), custom_call_target="tpu_custom_call" | custom-call | tf_op jit(solution)/shard_map/pallas_call | solution.py:252
  191.0 8.0 %collective-permute-done.18.via_a = bf16[768,384]{1,0:T(8,128)(2,1)S(1)} collective-permute-done((bf16[768,384]{1,0:T(8,128)(2,1)S(1)}, bf16[768,384]{1,0:T(8,128)(2,1)S(1)}, u32[]{:S(2)}, u32[]{:S(2)}) %collective-permute-start.18) | collective-permute-done | bytes 589856 | tf_op jit(solution)/shard_map/ppermute | solution.py:41
  199.1 2.3 add.53
  201.9 2.6 collective-permute-start.21
  204.6 25.4 %collective-permute-done.20 = bf16[1536,384]{1,0:T(8,128)(2,1)S(1)} collective-permute-done((bf16[1536,384]{1,0:T(8,128)(2,1)}, bf16[1536,384]{1,0:T(8,128)(2,1)S(1)}, u32[]{:S(2)}, u32[]{:S(2)}) %collective-permute-start.20) | collective-permute-done | bytes 1179680 | tf_op jit(solution)/shard_map/ppermute | solution.py:41
  231.4 10.5 %all-to-all-start.2 = ((bf16[64,24,384]{2,1,0:T(8,128)(2,1)}), bf16[64,24,384]{2,1,0:T(8,128)(2,1)S(1)}, u32[]{:S(2)}, u32[]{:S(2)}) async-start(bf16[64,24,384]{2,1,0:T(8,128)(2,1)} %bitcast.35), calls=%async_computation.2 | async-start | bytes 2359296 | tf_op jit(solution)/shard_map/all_to_all | solution.py:477
  243.5 12.8 %all_gather.7.late = bf16[128,2048]{1,0:T(8,128)(2,1)S(1)} all-gather(bf16[128,512]{1,0:T(8,128)(2,1)S(1)} %weigh.1), channel_id=1, replica_groups=mesh['section'=4,'dp'=8,'expert'=8] {'section'}, dimensions={1}, use_global_device_ids=true | all-gather | bytes 655360 | tf_op jit(solution)/shard_map/all_gather | solution.py:503
  256.4 16.8 %all-to-all-done.2 = bf16[64,24,384]{2,1,0:T(8,128)(2,1)S(1)} async-done(((bf16[64,24,384]{2,1,0:T(8,128)(2,1)}), bf16[64,24,384]{2,1,0:T(8,128)(2,1)S(1)}, u32[]{:S(2)}, u32[]{:S(2)}) %all-to-all-start.2) | async-done | bytes 1179680 | tf_op jit(solution)/shard_map/all_to_all | solution.py:477
  (97 shorter events, 28.3 us)
Async XLA Ops:
  1.0 14.0 %collective-permute-start.3 = (bf16[144,1152]{1,0:T(8,128)(2,1)S(1)}, bf16[144,1152]{1,0:T(8,128)(2,1)S(1)}, u32[]{:S(2)}, u32[]{:S(2)}) collective-permute-start(bf16[144,1152]{1,0:T(8,128)(2,1)S(1)} %constant_dynamic-slice_fusion), channel_id=1, source_target_pairs={{0,64},{64,128},{128,192},{192,0},{1,65},{65,129},{129,193},{193,1... | collective-permute-start | bytes 995336 | tf_op jit(solution)/shard_map/ppermute | solution.py:41
  2.6 18.5 %collective-permute-start.4 = (bf16[144,1152]{1,0:T(8,128)(2,1)S(1)}, bf16[144,1152]{1,0:T(8,128)(2,1)S(1)}, u32[]{:S(2)}, u32[]{:S(2)}) collective-permute-start(bf16[144,1152]{1,0:T(8,128)(2,1)S(1)} %constant_dynamic-slice_fusion), channel_id=1, source_target_pairs={{0,128},{64,192},{128,0},{192,64},{1,129},{65,193},{129,1},{193,65... | collective-permute-start | bytes 995336 | tf_op jit(solution)/shard_map/ppermute | solution.py:41
  5.3 18.1 %collective-permute-start.5 = (bf16[144,1152]{1,0:T(8,128)(2,1)S(1)}, bf16[144,1152]{1,0:T(8,128)(2,1)S(1)}, u32[]{:S(2)}, u32[]{:S(2)}) collective-permute-start(bf16[144,1152]{1,0:T(8,128)(2,1)S(1)} %constant_dynamic-slice_fusion), channel_id=1, source_target_pairs={{0,192},{64,0},{128,64},{192,128},{1,193},{65,1},{129,65},{193,129... | collective-permute-start | bytes 995336 | tf_op jit(solution)/shard_map/ppermute | solution.py:41
  6.7 42.0 %copy-start.17 = (s32[128,6]{0,1:T(8,128)S(1)}, s32[128,6]{0,1:T(8,128)}, u32[]{:S(2)}) copy-start(s32[128,6]{0,1:T(8,128)} %param.15) | copy-start | bytes 9220
  13.5 37.4 %copy-start = (bf16[512,1152]{1,0:T(8,128)(2,1)S(1)}, bf16[512,1152]{1,0:T(8,128)(2,1)}, u32[]{:S(2)}) copy-start(bf16[512,1152]{1,0:T(8,128)(2,1)} %patches.1) | copy-start | bytes 3538948
  13.5 37.4 %copy-start.1 = (bf16[288,1152]{1,0:T(8,128)(2,1)S(1)}, bf16[288,1152]{1,0:T(8,128)(2,1)}, u32[]{:S(2)}) copy-start(bf16[288,1152]{1,0:T(8,128)(2,1)} %refs_4_.1) | copy-start | bytes 1990660
  13.5 37.4 %copy-start.2 = (bf16[288,512]{1,0:T(8,128)(2,1)S(1)}, bf16[288,512]{1,0:T(8,128)(2,1)}, u32[]{:S(2)}) copy-start(bf16[288,512]{1,0:T(8,128)(2,1)} %attend.1.refs_0_) | copy-start | bytes 884740
  13.5 13.8 %collective-permute-start = (bf16[288,512]{1,0:T(8,128)(2,1)}, bf16[288,512]{1,0:T(8,128)(2,1)S(1)}, u32[]{:S(2)}, u32[]{:S(2)}) collective-permute-start(bf16[288,512]{1,0:T(8,128)(2,1)} %attend.1.refs_0_), channel_id=1, source_target_pairs={{0,64},{64,128},{128,192},{192,0},{1,65},{65,129},{129,193},{193,1... | collective-permute-start | bytes 884744 | tf_op jit(solution)/shard_map/ppermute | solution.py:41
  14.2 18.5 %collective-permute-start.1 = (bf16[288,512]{1,0:T(8,128)(2,1)}, bf16[288,512]{1,0:T(8,128)(2,1)S(1)}, u32[]{:S(2)}, u32[]{:S(2)}) collective-permute-start(bf16[288,512]{1,0:T(8,128)(2,1)} %attend.1.refs_0_), channel_id=1, source_target_pairs={{0,128},{64,192},{128,0},{192,64},{1,129},{65,193},{129,1},{193,65... | collective-permute-start | bytes 884744 | tf_op jit(solution)/shard_map/ppermute | solution.py:41
  15.0 27.1 %collective-permute-start.7 = (bf16[576,512]{1,0:T(8,128)(2,1)}, bf16[576,512]{1,0:T(8,128)(2,1)}, u32[]{:S(2)}, u32[]{:S(2)}) collective-permute-start(bf16[576,512]{1,0:T(8,128)(2,1)} %refs_9_.1), channel_id=1, source_target_pairs={{0,16},{8,24},{16,32},{24,40},{32,48},{40,56},{48,0},{56,8},{1,17}... | collective-permute-start | bytes 1769480 | tf_op jit(solution)/shard_map/ppermute | solution.py:41
  21.1 21.6 %collective-permute-start.8 = (bf16[576,512]{1,0:T(8,128)(2,1)}, bf16[576,512]{1,0:T(8,128)(2,1)}, u32[]{:S(2)}, u32[]{:S(2)}) collective-permute-start(bf16[576,512]{1,0:T(8,128)(2,1)} %refs_9_.1), channel_id=1, source_target_pairs={{0,32},{8,40},{16,48},{24,56},{32,0},{40,8},{48,16},{56,24},{1,33}... | collective-permute-start | bytes 1769480 | tf_op jit(solution)/shard_map/ppermute | solution.py:41
  23.4 25.2 %collective-permute-start.9 = (bf16[576,512]{1,0:T(8,128)(2,1)}, bf16[576,512]{1,0:T(8,128)(2,1)}, u32[]{:S(2)}, u32[]{:S(2)}) collective-permute-start(bf16[576,512]{1,0:T(8,128)(2,1)} %refs_9_.1), channel_id=1, source_target_pairs={{0,48},{8,56},{16,0},{24,8},{32,16},{40,24},{48,32},{56,40},{1,49}... | collective-permute-start | bytes 1769480 | tf_op jit(solution)/shard_map/ppermute | solution.py:41
  28.0 22.8 %collective-permute-start.6 = (bf16[432,1152]{1,0:T(8,128)(2,1)}, bf16[432,1152]{1,0:T(8,128)(2,1)}, u32[]{:S(2)}, u32[]{:S(2)}) collective-permute-start(bf16[432,1152]{1,0:T(8,128)(2,1)} %pad_maximum_fusion.1), channel_id=1, source_target_pairs={{0,8},{8,0},{16,24},{24,16},{32,40},{40,32},{48,56},{56,48},{1,9},... | collective-permute-start | bytes 2985992 | tf_op jit(solution)/shard_map/ppermute | solution.py:46
  33.3 8.1 %collective-permute-start.2 = (bf16[288,512]{1,0:T(8,128)(2,1)}, bf16[288,512]{1,0:T(8,128)(2,1)S(1)}, u32[]{:S(2)}, u32[]{:S(2)}) collective-permute-start(bf16[288,512]{1,0:T(8,128)(2,1)} %attend.1.refs_0_), channel_id=1, source_target_pairs={{0,192},{64,0},{128,64},{192,128},{1,193},{65,1},{129,65},{193,129... | collective-permute-start | bytes 884744 | tf_op jit(solution)/shard_map/ppermute | solution.py:41
  42.2 7.3 %collective-permute-start.10 = (bf16[576,512]{1,0:T(8,128)(2,1)}, bf16[576,512]{1,0:T(8,128)(2,1)S(1)}, u32[]{:S(2)}, u32[]{:S(2)}) collective-permute-start(bf16[576,512]{1,0:T(8,128)(2,1)} %refs_9_.1), channel_id=1, source_target_pairs={{0,8},{8,0},{16,24},{24,16},{32,40},{40,32},{48,56},{56,48},{1,9},... | collective-permute-start | bytes 1769480 | tf_op jit(solution)/shard_map/ppermute | solution.py:46
  42.2 7.3 %collective-permute-start.11 = (bf16[576,512]{1,0:T(8,128)(2,1)}, bf16[576,512]{1,0:T(8,128)(2,1)S(1)}, u32[]{:S(2)}, u32[]{:S(2)}) collective-permute-start(bf16[576,512]{1,0:T(8,128)(2,1)} %collective-permute-done.7.refs_10_), channel_id=1, source_target_pairs={{0,8},{8,0},{16,24},{24,16},{32,40},{40,32},{48,56},{56,48},{1,9},... | collective-permute-start | bytes 1769480 | tf_op jit(solution)/shard_map/ppermute | solution.py:46
  42.7 6.8 %collective-permute-start.12 = (bf16[576,512]{1,0:T(8,128)(2,1)}, bf16[576,512]{1,0:T(8,128)(2,1)S(1)}, u32[]{:S(2)}, u32[]{:S(2)}) collective-permute-start(bf16[576,512]{1,0:T(8,128)(2,1)} %collective-permute-done.8.refs_11_), channel_id=1, source_target_pairs={{0,8},{8,0},{16,24},{24,16},{32,40},{40,32},{48,56},{56,48},{1,9},... | collective-permute-start | bytes 1769480 | tf_op jit(solution)/shard_map/ppermute | solution.py:46
  48.6 2.2 collective-permute-start.13
  61.3 43.4 %all-to-all-start = ((bf16[64,24,384]{2,1,0:T(8,128)(2,1)}), bf16[64,24,384]{2,1,0:T(8,128)(2,1)}, u32[]{:S(2)}, u32[]{:S(2)}) async-start(bf16[64,24,384]{2,1,0:T(8,128)(2,1)} %bitcast.38), calls=%async_computation | async-start | bytes 2359296 | tf_op jit(solution)/shard_map/all_to_all | solution.py:477
  104.7 56.9 %all-to-all-start.1 = ((bf16[64,24,512]{2,1,0:T(8,128)(2,1)}), bf16[64,24,512]{2,1,0:T(8,128)(2,1)S(1)}, u32[]{:S(2)}, u32[]{:S(2)}) async-start(bf16[64,24,512]{2,1,0:T(8,128)(2,1)} %bitcast.30), calls=%async_computation.1 | async-start | bytes 3145728 | tf_op jit(solution)/shard_map/all_to_all | solution.py:477
  111.2 29.5 %collective-permute-start.14 = (bf16[1536,384]{1,0:T(8,128)(2,1)}, bf16[1536,384]{1,0:T(8,128)(2,1)S(1)}, u32[]{:S(2)}, u32[]{:S(2)}) collective-permute-start(bf16[1536,384]{1,0:T(8,128)(2,1)} %bitcast.5.own), channel_id=1, source_target_pairs={{0,64},{64,128},{128,192},{192,0},{1,65},{65,129},{129,193},{193,1... | collective-permute-start | bytes 3538952 | tf_op jit(solution)/shard_map/ppermute | solution.py:41
  111.3 29.4 %collective-permute-start.15 = (bf16[1536,384]{1,0:T(8,128)(2,1)}, bf16[1536,384]{1,0:T(8,128)(2,1)S(1)}, u32[]{:S(2)}, u32[]{:S(2)}) collective-permute-start(bf16[1536,384]{1,0:T(8,128)(2,1)} %bitcast.5.own), channel_id=1, source_target_pairs={{0,192},{64,0},{128,64},{192,128},{1,193},{65,1},{129,65},{193,129... | collective-permute-start | bytes 3538952 | tf_op jit(solution)/shard_map/ppermute | solution.py:41
  115.6 33.4 %copy-start.12 = (bf16[1,2048,352]{1,2,0:T(8,128)(2,1)S(1)}, bf16[1,2048,352]{1,2,0:T(8,128)(2,1)}, u32[]{:S(2)}) copy-start(bf16[1,2048,352]{1,2,0:T(8,128)(2,1)} %param.18) | copy-start | bytes 4325380
  145.0 16.6 %collective-permute-start.16 = (bf16[768,384]{1,0:T(8,128)(2,1)}, bf16[768,384]{1,0:T(8,128)(2,1)}, u32[]{:S(2)}, u32[]{:S(2)}) collective-permute-start(bf16[768,384]{1,0:T(8,128)(2,1)} %get-tuple-element.25), channel_id=1, source_target_pairs={{0,64},{64,128},{128,192},{192,0},{1,65},{65,129},{129,193},{193,1... | collective-permute-start | bytes 1769480 | tf_op jit(solution)/shard_map/ppermute | solution.py:41
  145.0 16.6 %collective-permute-start.17 = (bf16[768,384]{1,0:T(8,128)(2,1)}, bf16[768,384]{1,0:T(8,128)(2,1)}, u32[]{:S(2)}, u32[]{:S(2)}) collective-permute-start(bf16[768,384]{1,0:T(8,128)(2,1)} %get-tuple-element.26), channel_id=1, source_target_pairs={{0,192},{64,0},{128,64},{192,128},{1,193},{65,1},{129,65},{193,129... | collective-permute-start | bytes 1769480 | tf_op jit(solution)/shard_map/ppermute | solution.py:41
  171.9 59.5 %all-to-all-start.3 = ((bf16[64,24,512]{2,1,0:T(8,128)(2,1)}), bf16[64,24,512]{2,1,0:T(8,128)(2,1)S(1)}, u32[]{:S(2)}, u32[]{:S(2)}) async-start(bf16[64,24,512]{2,1,0:T(8,128)(2,1)} %bitcast.37), calls=%async_computation.3 | async-start | bytes 3145728 | tf_op jit(solution)/shard_map/all_to_all | solution.py:477
  182.4 16.7 %collective-permute-start.18 = (bf16[768,384]{1,0:T(8,128)(2,1)S(1)}, bf16[768,384]{1,0:T(8,128)(2,1)S(1)}, u32[]{:S(2)}, u32[]{:S(2)}) collective-permute-start(bf16[768,384]{1,0:T(8,128)(2,1)S(1)} %copy-done.22), channel_id=1, source_target_pairs={{0,64},{64,128},{128,192},{192,0},{1,65},{65,129},{129,193},{193,1... | collective-permute-start | bytes 1769480 | tf_op jit(solution)/shard_map/ppermute | solution.py:41
  182.5 16.6 %collective-permute-start.19 = (bf16[768,384]{1,0:T(8,128)(2,1)S(1)}, bf16[768,384]{1,0:T(8,128)(2,1)S(1)}, u32[]{:S(2)}, u32[]{:S(2)}) collective-permute-start(bf16[768,384]{1,0:T(8,128)(2,1)S(1)} %copy-done.21), channel_id=1, source_target_pairs={{0,192},{64,0},{128,64},{192,128},{1,193},{65,1},{129,65},{193,129... | collective-permute-start | bytes 1769480 | tf_op jit(solution)/shard_map/ppermute | solution.py:41
  199.1 30.9 %copy-start.16 = (bf16[1536,384]{1,0:T(8,128)(2,1)S(1)}, bf16[1536,384]{1,0:T(8,128)(2,1)}, u32[]{:S(2)}) copy-start(bf16[1536,384]{1,0:T(8,128)(2,1)} %get-tuple-element.28) | copy-start | bytes 3538948
  201.3 28.6 %collective-permute-start.20 = (bf16[1536,384]{1,0:T(8,128)(2,1)}, bf16[1536,384]{1,0:T(8,128)(2,1)S(1)}, u32[]{:S(2)}, u32[]{:S(2)}) collective-permute-start(bf16[1536,384]{1,0:T(8,128)(2,1)} %get-tuple-element.33), channel_id=1, source_target_pairs={{0,64},{64,128},{128,192},{192,0},{1,65},{65,129},{129,193},{193,1... | collective-permute-start | bytes 3538952 | tf_op jit(solution)/shard_map/ppermute | solution.py:41
  201.9 28.0 %collective-permute-start.21 = (bf16[1536,384]{1,0:T(8,128)(2,1)}, bf16[1536,384]{1,0:T(8,128)(2,1)S(1)}, u32[]{:S(2)}, u32[]{:S(2)}) collective-permute-start(bf16[1536,384]{1,0:T(8,128)(2,1)} %get-tuple-element.34), channel_id=1, source_target_pairs={{0,192},{64,0},{128,64},{192,128},{1,193},{65,1},{129,65},{193,129... | collective-permute-start | bytes 3538952 | tf_op jit(solution)/shard_map/ppermute | solution.py:41
  231.4 41.7 %all-to-all-start.2 = ((bf16[64,24,384]{2,1,0:T(8,128)(2,1)}), bf16[64,24,384]{2,1,0:T(8,128)(2,1)S(1)}, u32[]{:S(2)}, u32[]{:S(2)}) async-start(bf16[64,24,384]{2,1,0:T(8,128)(2,1)} %bitcast.35), calls=%async_computation.2 | async-start | bytes 2359296 | tf_op jit(solution)/shard_map/all_to_all | solution.py:477
  (17 other events, 79.0 us)
